TPU v7x, 32 devices: a whole 2x2x4 slice. The times are simulated.
32 devices in a mesh: ta: 4 (over x, core), ha: 2 (over y), col: 4 (over z).
Axes of the slice: x: 2, y: 2, z: 4, core: 2. Of those that a mesh axis runs over, the one named last changes fastest.
Arguments:
- tokens: bfloat16 [8, 32, 14, 14, 512], P('col', 'ta', 'ha'), may hold values from -6 to 6
- qkv_weight: bfloat16 [512, 1536], P('col', ('ta', 'ha')), may hold values from -0.25 to 0.25
- query_bias: bfloat16 [512], P(('ta', 'ha')), may hold values from -2 to 2
- value_bias: bfloat16 [512], P(('ta', 'ha')), may hold values from -0.59765625 to 0.59765625
- proj_weight: bfloat16 [512, 512], P('col', ('ta', 'ha')), may hold values from -2 to 2
- proj_bias: bfloat16 [512], P(('ta', 'ha')), may hold values from -2 to 2
- fc1_weight: bfloat16 [512, 2048], P('col', ('ta', 'ha')), may hold values from -0.25 to 0.25
- fc1_bias: bfloat16 [2048], P(('ta', 'ha')), may hold values from -2 to 2
- fc2_weight: bfloat16 [2048, 512], P('col', ('ta', 'ha')), may hold values from -0.125 to 0.125
- fc2_bias: bfloat16 [512], P(('ta', 'ha')), may hold values from -2 to 2
- norm1_gain: bfloat16 [512], P(('ta', 'ha')), may hold values from 0.5 to 1.5
- norm1_shift: bfloat16 [512], P(('ta', 'ha')), may hold values from -1.1953125 to 1.1953125
- norm2_gain: bfloat16 [512], P(('ta', 'ha')), may hold values from 0.5 to 1.5
- norm2_shift: bfloat16 [512], P(('ta', 'ha')), may hold values from -1.1953125 to 1.1953125
- bias_table: bfloat16 [2535, 16], P(None, ('ta', 'ha')), may hold values from -3 to 3
- rel_index: int32 [392, 392], replicated, may hold values from 0 to 2534, as said below
- cotangent: bfloat16 [8, 32, 14, 14, 512], P('col', 'ta', 'ha'), may hold values from -6 to 6
Outputs:
- block_out: bfloat16 [8, 32, 14, 14, 512], P('col', 'ta', 'ha')
- tokens_grad: float32 [8, 32, 14, 14, 512], P('col', 'ta', 'ha')
- qkv_weight_grad: float32 [512, 1536], P(None, ('ta', 'ha'))
- query_bias_grad: float32 [512], P(('ta', 'ha'))
- value_bias_grad: float32 [512], P(('ta', 'ha'))
- proj_weight_grad: float32 [512, 512], P(None, ('ta', 'ha'))
- proj_bias_grad: float32 [512], P(('ta', 'ha'))
- fc1_weight_grad: float32 [512, 2048], P(None, ('ta', 'ha'))
- fc1_bias_grad: float32 [2048], P(('ta', 'ha'))
- fc2_weight_grad: float32 [2048, 512], P(None, ('ta', 'ha'))
- fc2_bias_grad: float32 [512], P(('ta', 'ha'))
- norm1_gain_grad: float32 [512], P(('ta', 'ha'))
- norm1_shift_grad: float32 [512], P(('ta', 'ha'))
- norm2_gain_grad: float32 [512], P(('ta', 'ha'))
- norm2_shift_grad: float32 [512], P(('ta', 'ha'))
- bias_table_grad: float32 [2535, 16], P(None, ('ta', 'ha'))
Inputs may be any that keep to these rules, and one draw needn't show every extreme that they name: `rel_index`: entry (i, j) depends only on the differences of the frame, row and column of positions i and j inside a window, and distinct differences name distinct rows of bias_table.
All inputs are finite; a program needn't handle non-finite values.
Results may differ from a plain program's by a relative error of at most 0.012.
Values may be sent and summed in bfloat16 or wider, within the bound.
No kernel may reach another device: no remote copies, remote signals or barrier semaphores. Data moves between devices by JAX's collectives and lax.ppermute only.
A program may use at most 256 MiB of HBM per device.

v0:
```python
import jax
import jax.numpy as jnp
from jax import lax
from jax.sharding import PartitionSpec as P

D = 512
HEADS = 16
WIN_T = 8
WIN_H = 7
WIN_W = 7
HEAD_DIM = 32
SHIFT_T = 4
SHIFT_H = 3
SHIFT_W = 3
WIDTH = 14
WIN = 392
RPB_ROWS = 2535


def passed_along(value, axis, by):
    devices = lax.axis_size(axis)
    return lax.ppermute(value, axis, [(i, (i + by) % devices) for i in range(devices)])


def norm_rows(values, norm_gain, norm_shift):
    centre = values - jnp.mean(values, axis=-1, keepdims=True)
    inv_std = lax.rsqrt(jnp.mean(centre * centre, axis=-1, keepdims=True) + 1e-05)
    normed = centre * inv_std
    return (normed, inv_std, normed * norm_gain + norm_shift)


def norm_back(grad_out, normed, inv_std, norm_gain):
    scaled = grad_out * norm_gain
    return inv_std * (
        scaled
        - jnp.mean(scaled, axis=-1, keepdims=True)
        - normed * jnp.mean(scaled * normed, axis=-1, keepdims=True)
    )


def gelu_slope(values):
    normal_cdf = 0.5 * (1.0 + lax.erf(values * 0.7071067811865476))
    return normal_cdf + values * jnp.exp(-0.5 * values * values) * 0.3989422804014327


def to_windows(token_rows, clip_count):
    width = token_rows.shape[-1]
    blocks = token_rows.reshape(clip_count, WIN_T, WIN_H, WIDTH // WIN_W, WIN_W, width)
    return blocks.transpose(0, 3, 1, 2, 4, 5).reshape(-1, WIN, width)


def from_windows(windows, clip_count):
    width = windows.shape[-1]
    blocks = windows.reshape(clip_count, WIDTH // WIN_W, WIN_T, WIN_H, WIN_W, width)
    return blocks.transpose(0, 2, 3, 1, 4, 5).reshape(-1, width)


def into_rolled(leading, trailing):
    arrived = passed_along((leading[:, :SHIFT_T], trailing[:, :SHIFT_T]), "ta", -1)
    leading_t = jnp.concatenate([leading[:, SHIFT_T:], arrived[0]], axis=1)
    trailing_t = jnp.concatenate([trailing[:, SHIFT_T:], arrived[1]], axis=1)
    arrived_rows = passed_along((leading_t[:, :, :SHIFT_H], trailing_t[:, :, :SHIFT_H]), "ha", -1)
    leading_r = jnp.roll(
        jnp.concatenate([leading_t[:, :, SHIFT_H:], arrived_rows[0]], axis=2), -SHIFT_W, axis=3
    )
    trailing_r = jnp.roll(
        jnp.concatenate([trailing_t[:, :, SHIFT_H:], arrived_rows[1]], axis=2), -SHIFT_W, axis=3
    )
    return (leading_r, trailing_r)


def out_of_rolled(leading, trailing):
    leading_w = jnp.roll(leading, SHIFT_W, axis=3)
    trailing_w = jnp.roll(trailing, SHIFT_W, axis=3)
    arrived_rows = (
        passed_along(leading_w[:, :, WIN_H - SHIFT_H :].astype(jnp.bfloat16), "ha", 1).astype(
            jnp.float32
        ),
        passed_along(trailing_w[:, :, WIN_H - SHIFT_H :].astype(jnp.bfloat16), "ha", 1).astype(
            jnp.float32
        ),
    )
    leading_h = jnp.concatenate([arrived_rows[0], leading_w[:, :, : WIN_H - SHIFT_H]], axis=2)
    trailing_h = jnp.concatenate([arrived_rows[1], trailing_w[:, :, : WIN_H - SHIFT_H]], axis=2)
    arrived = (
        passed_along(leading_h[:, WIN_T - SHIFT_T :].astype(jnp.bfloat16), "ta", 1).astype(
            jnp.float32
        ),
        passed_along(trailing_h[:, WIN_T - SHIFT_T :].astype(jnp.bfloat16), "ta", 1).astype(
            jnp.float32
        ),
    )
    leading_o = jnp.concatenate([arrived[0], leading_h[:, : WIN_T - SHIFT_T]], axis=1)
    trailing_o = jnp.concatenate([arrived[1], trailing_h[:, : WIN_T - SHIFT_T]], axis=1)
    return (leading_o, trailing_o)


def gather_weights(
    qkv_weight,
    proj_weight,
    fc1_weight,
    fc2_weight,
    query_bias,
    value_bias,
    proj_bias,
    fc1_bias,
    fc2_bias,
    norm1_gain,
    norm1_shift,
    norm2_gain,
    norm2_shift,
    bias_table,
):
    col_whole = (
        lax.all_gather(qkv_weight, "col", axis=0, tiled=True),
        lax.all_gather(proj_weight, "col", axis=0, tiled=True),
        lax.all_gather(fc1_weight, "col", axis=0, tiled=True),
        lax.all_gather(fc2_weight, "col", axis=0, tiled=True),
    )
    return (
        lax.all_gather(col_whole[0], ("ta", "ha"), axis=1, tiled=True),
        lax.all_gather(col_whole[1], ("ta", "ha"), axis=1, tiled=True),
        lax.all_gather(col_whole[2], ("ta", "ha"), axis=1, tiled=True),
        lax.all_gather(col_whole[3], ("ta", "ha"), axis=1, tiled=True),
        lax.all_gather(query_bias, ("ta", "ha"), axis=0, tiled=True),
        lax.all_gather(value_bias, ("ta", "ha"), axis=0, tiled=True),
        lax.all_gather(proj_bias, ("ta", "ha"), axis=0, tiled=True),
        lax.all_gather(fc1_bias, ("ta", "ha"), axis=0, tiled=True),
        lax.all_gather(fc2_bias, ("ta", "ha"), axis=0, tiled=True),
        lax.all_gather(norm1_gain, ("ta", "ha"), axis=0, tiled=True),
        lax.all_gather(norm1_shift, ("ta", "ha"), axis=0, tiled=True),
        lax.all_gather(norm2_gain, ("ta", "ha"), axis=0, tiled=True),
        lax.all_gather(norm2_shift, ("ta", "ha"), axis=0, tiled=True),
        lax.all_gather(bias_table, ("ta", "ha"), axis=1, tiled=True),
    )


def gather_again(qkv_weight, proj_weight, fc1_weight, fc2_weight):
    col_whole = (
        lax.all_gather(qkv_weight, "col", axis=0, tiled=True),
        lax.all_gather(proj_weight, "col", axis=0, tiled=True),
        lax.all_gather(fc1_weight, "col", axis=0, tiled=True),
        lax.all_gather(fc2_weight, "col", axis=0, tiled=True),
    )
    return (
        lax.all_gather(col_whole[0], ("ta", "ha"), axis=1, tiled=True),
        lax.all_gather(col_whole[1], ("ta", "ha"), axis=1, tiled=True),
        lax.all_gather(col_whole[2], ("ta", "ha"), axis=1, tiled=True),
        lax.all_gather(col_whole[3], ("ta", "ha"), axis=1, tiled=True),
    )


def per_device(
    tokens,
    qkv_weight,
    query_bias,
    value_bias,
    proj_weight,
    proj_bias,
    fc1_weight,
    fc1_bias,
    fc2_weight,
    fc2_bias,
    norm1_gain,
    norm1_shift,
    norm2_gain,
    norm2_shift,
    bias_table,
    rel_index,
    cotangent,
):
    clip_count = tokens.shape[0]
    moved_in = into_rolled(tokens, cotangent)
    collected = gather_weights(
        qkv_weight,
        proj_weight,
        fc1_weight,
        fc2_weight,
        query_bias,
        value_bias,
        proj_bias,
        fc1_bias,
        fc2_bias,
        norm1_gain,
        norm1_shift,
        norm2_gain,
        norm2_shift,
        bias_table,
    )
    full_qkv, full_proj, full_fc1, full_fc2 = (
        collected[0],
        collected[1],
        collected[2],
        collected[3],
    )
    bias_query = collected[4].astype(jnp.float32)
    bias_value = collected[5].astype(jnp.float32)
    bias_proj = collected[6].astype(jnp.float32)
    bias_fc1 = collected[7].astype(jnp.float32)
    bias_fc2 = collected[8].astype(jnp.float32)
    gain_one = collected[9].astype(jnp.float32)
    shift_one = collected[10].astype(jnp.float32)
    gain_two = collected[11].astype(jnp.float32)
    shift_two = collected[12].astype(jnp.float32)
    table_full = collected[13].astype(jnp.float32)
    frames_all = WIN_T * lax.axis_size("ta")
    rows_all = WIN_H * lax.axis_size("ha")
    frame_pos = lax.axis_index("ta") * WIN_T + jnp.arange(WIN_T, dtype=jnp.int32)
    row_pos = lax.axis_index("ha") * WIN_H + jnp.arange(WIN_H, dtype=jnp.int32)
    column_pos = jnp.arange(WIDTH, dtype=jnp.int32)
    frame_reg = (frame_pos >= frames_all - WIN_T).astype(jnp.int32) + (
        frame_pos >= frames_all - SHIFT_T
    ).astype(jnp.int32)
    row_reg = (row_pos >= rows_all - WIN_H).astype(jnp.int32) + (
        row_pos >= rows_all - SHIFT_H
    ).astype(jnp.int32)
    column_reg = (column_pos >= WIDTH - WIN_W).astype(jnp.int32) + (
        column_pos >= WIDTH - SHIFT_W
    ).astype(jnp.int32)
    region_grid = (
        frame_reg[:, None, None] * 9 + row_reg[None, :, None] * 3 + column_reg[None, None, :]
    )
    region_one = (
        region_grid.reshape(WIN_T, WIN_H, WIDTH // WIN_W, WIN_W)
        .transpose(2, 0, 1, 3)
        .reshape(-1, WIN)
    )
    region_win = jnp.tile(region_one, (clip_count, 1))
    position_bias = table_full[rel_index].transpose(2, 0, 1)

    def window_scores(query_win, key_win, region):
        query_head = query_win.reshape(WIN, HEADS, HEAD_DIM)
        key_head = key_win.reshape(WIN, HEADS, HEAD_DIM)
        logits = jnp.einsum(
            "qhd,khd->hqk", query_head, key_head, preferred_element_type=jnp.float32
        )
        masked = jnp.where(region[:, None] != region[None, :], -100.0, 0.0).astype(jnp.float32)
        return logits * HEAD_DIM ** (-0.5) + position_bias + masked

    def attend_forward(inputs):
        query_win, key_win, value_win, region = inputs
        logits = window_scores(query_win, key_win, region)
        highest = jnp.max(logits, axis=-1, keepdims=True)
        exponent = jnp.exp(logits - highest)
        denominator = jnp.sum(exponent, axis=-1, keepdims=True)
        weights = (exponent / denominator).astype(jnp.bfloat16)
        value_head = value_win.reshape(WIN, HEADS, HEAD_DIM)
        mixture = jnp.einsum(
            "hqk,khd->qhd", weights, value_head, preferred_element_type=jnp.float32
        )
        log_norm = highest[..., 0] + jnp.log(denominator[..., 0])
        return (mixture.reshape(WIN, D).astype(jnp.bfloat16), log_norm)

    def attend_backward(running, inputs):
        query_win, key_win, value_win, region, log_norm, grad_win = inputs
        logits = window_scores(query_win, key_win, region)
        probability = jnp.exp(logits - log_norm[..., None])
        query_head = query_win.reshape(WIN, HEADS, HEAD_DIM)
        key_head = key_win.reshape(WIN, HEADS, HEAD_DIM)
        value_head = value_win.reshape(WIN, HEADS, HEAD_DIM)
        grad_head = grad_win.reshape(WIN, HEADS, HEAD_DIM)
        grad_prob = jnp.einsum(
            "qhd,khd->hqk", grad_head, value_head, preferred_element_type=jnp.float32
        )
        grad_value = jnp.einsum(
            "hqk,qhd->khd",
            probability.astype(jnp.bfloat16),
            grad_head,
            preferred_element_type=jnp.float32,
        )
        grad_logits = probability * (
            grad_prob - jnp.sum(probability * grad_prob, axis=-1, keepdims=True)
        )
        scaled = (grad_logits * HEAD_DIM ** (-0.5)).astype(jnp.bfloat16)
        grad_query = jnp.einsum(
            "hqk,khd->qhd", scaled, key_head, preferred_element_type=jnp.float32
        )
        grad_key = jnp.einsum(
            "hqk,qhd->khd", scaled, query_head, preferred_element_type=jnp.float32
        )
        return (
            running + grad_logits,
            (
                grad_query.reshape(WIN, D).astype(jnp.bfloat16),
                grad_key.reshape(WIN, D).astype(jnp.bfloat16),
                grad_value.reshape(WIN, D).astype(jnp.bfloat16),
            ),
        )

    x_rows = moved_in[0].reshape(-1, D).astype(jnp.float32)
    normed_one, inv_one, pre_one = norm_rows(x_rows, gain_one, shift_one)
    entry_rows = pre_one.astype(jnp.bfloat16)
    projected = jnp.dot(entry_rows, full_qkv, preferred_element_type=jnp.float32)
    queries = (projected[:, :D] + bias_query).astype(jnp.bfloat16)
    keys_rows = projected[:, D : 2 * D].astype(jnp.bfloat16)
    values_rows = (projected[:, 2 * D :] + bias_value).astype(jnp.bfloat16)
    query_wins = to_windows(queries, clip_count)
    key_wins = to_windows(keys_rows, clip_count)
    value_wins = to_windows(values_rows, clip_count)
    mixture_wins, log_norms = lax.map(
        attend_forward, (query_wins, key_wins, value_wins, region_win)
    )
    mixture_rows = from_windows(mixture_wins, clip_count)
    attention = jnp.dot(mixture_rows, full_proj, preferred_element_type=jnp.float32)
    middle = x_rows + (attention + bias_proj)
    normed_two, inv_two, pre_two = norm_rows(middle, gain_two, shift_two)
    second = pre_two.astype(jnp.bfloat16)
    hidden = jnp.dot(second, full_fc1, preferred_element_type=jnp.float32) + bias_fc1
    activation = jax.nn.gelu(hidden, approximate=False).astype(jnp.bfloat16)
    result = middle + (jnp.dot(activation, full_fc2, preferred_element_type=jnp.float32) + bias_fc2)
    back_qkv, back_proj, back_fc1, back_fc2 = gather_again(
        qkv_weight, proj_weight, fc1_weight, fc2_weight
    )
    grad_out = moved_in[1].reshape(-1, D)
    grad_fc2_bias = jnp.sum(grad_out.astype(jnp.float32), axis=0)
    grad_fc2 = jnp.einsum("nf,nd->fd", activation, grad_out, preferred_element_type=jnp.float32)
    grad_act = jnp.einsum("nd,fd->nf", grad_out, back_fc2, preferred_element_type=jnp.float32)
    grad_hidden = grad_act * gelu_slope(hidden)
    grad_fc1_bias = jnp.sum(grad_hidden, axis=0)
    hidden_low = grad_hidden.astype(jnp.bfloat16)
    grad_fc1 = jnp.einsum("nd,nf->df", second, hidden_low, preferred_element_type=jnp.float32)
    grad_second = jnp.einsum("nf,df->nd", hidden_low, back_fc1, preferred_element_type=jnp.float32)
    grad_gain_two = jnp.sum(grad_second * normed_two, axis=0)
    grad_shift_two = jnp.sum(grad_second, axis=0)
    grad_middle = grad_out.astype(jnp.float32) + norm_back(
        grad_second, normed_two, inv_two, gain_two
    )
    grad_proj_bias = jnp.sum(grad_middle, axis=0)
    middle_low = grad_middle.astype(jnp.bfloat16)
    grad_proj = jnp.einsum(
        "nd,ne->de", mixture_rows, middle_low, preferred_element_type=jnp.float32
    )
    grad_mixture = jnp.einsum(
        "ne,de->nd", middle_low, back_proj, preferred_element_type=jnp.float32
    ).astype(jnp.bfloat16)
    table_terms, window_grads = lax.scan(
        attend_backward,
        jnp.zeros((HEADS, WIN, WIN), jnp.float32),
        (
            query_wins,
            key_wins,
            value_wins,
            region_win,
            log_norms,
            to_windows(grad_mixture, clip_count),
        ),
    )
    grad_table = jax.ops.segment_sum(
        table_terms.transpose(1, 2, 0).reshape(WIN * WIN, HEADS),
        rel_index.reshape(-1),
        num_segments=RPB_ROWS,
    )
    grad_queries = from_windows(window_grads[0], clip_count)
    grad_keys = from_windows(window_grads[1], clip_count)
    grad_values = from_windows(window_grads[2], clip_count)
    grad_query_bias = jnp.sum(grad_queries.astype(jnp.float32), axis=0)
    grad_value_bias = jnp.sum(grad_values.astype(jnp.float32), axis=0)
    grad_projected = jnp.concatenate([grad_queries, grad_keys, grad_values], axis=1)
    grad_qkv = jnp.einsum(
        "nd,ne->de", entry_rows, grad_projected, preferred_element_type=jnp.float32
    )
    grad_entry = jnp.einsum(
        "ne,de->nd", grad_projected, back_qkv, preferred_element_type=jnp.float32
    )
    grad_gain_one = jnp.sum(grad_entry * normed_one, axis=0)
    grad_shift_one = jnp.sum(grad_entry, axis=0)
    grad_tokens = grad_middle + norm_back(grad_entry, normed_one, inv_one, gain_one)
    grid_shape = (clip_count, WIN_T, WIN_H, WIDTH, D)
    moved_out = out_of_rolled(result.reshape(grid_shape), grad_tokens.reshape(grid_shape))
    shares = (
        lax.psum_scatter(grad_qkv, ("ta", "ha"), scatter_dimension=1, tiled=True),
        lax.psum_scatter(grad_query_bias, ("ta", "ha"), scatter_dimension=0, tiled=True),
        lax.psum_scatter(grad_value_bias, ("ta", "ha"), scatter_dimension=0, tiled=True),
        lax.psum_scatter(grad_proj, ("ta", "ha"), scatter_dimension=1, tiled=True),
        lax.psum_scatter(grad_proj_bias, ("ta", "ha"), scatter_dimension=0, tiled=True),
        lax.psum_scatter(grad_fc1, ("ta", "ha"), scatter_dimension=1, tiled=True),
        lax.psum_scatter(grad_fc1_bias, ("ta", "ha"), scatter_dimension=0, tiled=True),
        lax.psum_scatter(grad_fc2, ("ta", "ha"), scatter_dimension=1, tiled=True),
        lax.psum_scatter(grad_fc2_bias, ("ta", "ha"), scatter_dimension=0, tiled=True),
        lax.psum_scatter(grad_gain_one, ("ta", "ha"), scatter_dimension=0, tiled=True),
        lax.psum_scatter(grad_shift_one, ("ta", "ha"), scatter_dimension=0, tiled=True),
        lax.psum_scatter(grad_gain_two, ("ta", "ha"), scatter_dimension=0, tiled=True),
        lax.psum_scatter(grad_shift_two, ("ta", "ha"), scatter_dimension=0, tiled=True),
        lax.psum_scatter(grad_table, ("ta", "ha"), scatter_dimension=1, tiled=True),
    )
    totals = lax.psum(
        (
            shares[0],
            shares[1],
            shares[2],
            shares[3],
            shares[4],
            shares[5],
            shares[6],
            shares[7],
            shares[8],
            shares[9],
            shares[10],
            shares[11],
            shares[12],
            shares[13],
        ),
        "col",
    )
    return (
        moved_out[0].astype(jnp.bfloat16),
        moved_out[1],
        totals[0],
        totals[1],
        totals[2],
        totals[3],
        totals[4],
        totals[5],
        totals[6],
        totals[7],
        totals[8],
        totals[9],
        totals[10],
        totals[11],
        totals[12],
        totals[13],
    )


def solution(mesh):
    placed = (
        P("col", "ta", "ha", None, None),
        P("col", ("ta", "ha")),
        P(("ta", "ha")),
        P(("ta", "ha")),
        P("col", ("ta", "ha")),
        P(("ta", "ha")),
        P("col", ("ta", "ha")),
        P(("ta", "ha")),
        P("col", ("ta", "ha")),
        P(("ta", "ha")),
        P(("ta", "ha")),
        P(("ta", "ha")),
        P(("ta", "ha")),
        P(("ta", "ha")),
        P(None, ("ta", "ha")),
        P(),
        P("col", "ta", "ha", None, None),
    )
    return jax.shard_map(
        per_device,
        mesh=mesh,
        in_specs=placed,
        out_specs=(
            P("col", "ta", "ha", None, None),
            P("col", "ta", "ha", None, None),
            P(None, ("ta", "ha")),
            P(("ta", "ha")),
            P(("ta", "ha")),
            P(None, ("ta", "ha")),
            P(("ta", "ha")),
            P(None, ("ta", "ha")),
            P(("ta", "ha")),
            P(None, ("ta", "ha")),
            P(("ta", "ha")),
            P(("ta", "ha")),
            P(("ta", "ha")),
            P(("ta", "ha")),
            P(("ta", "ha")),
            P(None, ("ta", "ha")),
        ),
        check_vma=False,
    )
```

profile of v0, /device:TPU:0, one launch (start us, length us, event | category | flops | bytes accessed | tf_op | source)
XLA Modules:
  0.0 2134.0 jit_solution(1294760514916189454)
XLA Ops:
  7.2 16.1 all_gather.64
  23.4 15.2 all_gather.74
  47.0 15.0 all_gather.77
  68.8 14.8 all-reduce.21
  86.5 15.4 all-gather
  102.3 282.6 %gather_fusion = f32[153664,16]{1,0:T(8,128)} fusion(f32[2535,16]{1,0:T(8,128)S(1)} %bitcast.174, s32[154624]{0:T(1024)S(1)} %pad_clamp_fusion), kind=kCustom, calls=%fused_computation | custom fusion | bytes 20283648 | tf_op jit(solution)/shard_map/gather | solution.py:229
  384.9 54.6 %copy.231 = f32[392,392,16]{0,1,2:T(8,128)} copy(f32[392,392,16]{2,1,0:T(8,128)} %bitcast.14) | data formatting | bytes 19668992 | tf_op jit(solution)/shard_map/gather | solution.py:229
  443.9 25.0 %all-gather.1 = bf16[8,1,256]{2,1,0:T(2,128)(2,1)S(1)} all-gather(bf16[1,1,256]{2,1,0:T(2,128)(2,1)S(1)} %reshape.466), channel_id=1, replica_groups=mesh['ta'=4,'ha'=2,'col'=4] {'ta','ha'}, dimensions={0}, use_global_device_ids=true | all-gather | bytes 4608 | tf_op jit(solution)/shard_map/all_gather | solution.py:128
  470.6 12.1 all_gather.69
  482.8 28.9 %all_gather.70 = bf16[512,512]{0,1:T(8,128)(2,1)} all-gather(bf16[512,64]{0,1:T(8,128)(2,1)S(1)} %all_gather.69), channel_id=1, replica_groups=mesh['ta'=4,'ha'=2,'col'=4] {'ta','ha'}, dimensions={1}, use_global_device_ids=true | all-gather | bytes 589824 | tf_op jit(solution)/shard_map/all_gather | solution.py:122
  593.3 55.6 %while.29 = (s32[]{:T(128)}, bf16[4,392,512]{1,2,0:T(8,128)(2,1)}, f32[4,16,392]{2,1,0:T(8,128)}, bf16[4,392,512]{1,2,0:T(8,128)(2,1)S(1)}, bf16[4,392,512]{1,2,...) while((s32[]{:T(128)}, bf16[4,392,512]{1,2,0:T(8,128)(2,1)}, ...), condition=%wide.region_5.6_spmd, body=%wide.region_2.5_spmd.sunk | while | flops 337333248 | bytes 45720280 | solution.py:300
  665.8 34.1 %fusion.44 = (bf16[1568,2048]{1,0:T(8,128)(2,1)}, f32[1568,2048]{1,0:T(8,128)}) fusion(f32[2048]{0:T(1024)S(1)} %bitcast.210, bf16[512,2048]{1,0:T(8,128)(2,1)} %all-gather.8.cloned.1.call-done, f32[1568,512]{1,0:T(8,128)S(1)} %get-tuple-element.449, f32[512]{0:T(512)S(1)} %copy-done.58, f32[512]{0:T(512)S(1)} %copy-done.44, f32[1568]{0:T(1024)S(1)} %add_rsqrt_fusion, ...), kind=kOutput, calls=%fused_computation.48 | convolution fusion | flops 3504291840 | bytes 24600832 | tf_op jit(solution)/shard_map/dot_general | solution.py:308
  700.0 11.9 fusion.98
  733.7 268.0 %while.30 = (s32[]{:T(128)}, f32[16,392,392]{1,2,0:T(8,128)}, bf16[4,392,512]{1,2,0:T(8,128)(2,1)}, bf16[4,392,512]{1,2,0:T(8,128)(2,1)}, bf16[4,392,512]{1,2,0:...) while((s32[]{:T(128)}, f32[16,392,392]{1,2,0:T(8,128)}, ...), condition=%wide.region_12.13_spmd.clone, body=%wide.region_10.12_spmd.clone.sunk | while | flops 1623621248 | bytes 91593496 | solution.py:336
  737.1 9.3 subtract_exponential_fusion.3
  748.6 14.7 select_add_fusion.2
  763.3 12.9 fusion.201
  783.6 13.5 fusion.203
  801.2 9.3 subtract_exponential_fusion.3
  812.7 18.4 select_add_fusion.2
  831.1 12.9 fusion.201
  851.4 13.5 fusion.203
  880.5 18.4 select_add_fusion.2
  898.9 12.9 fusion.201
  919.3 13.5 fusion.203
  948.3 18.4 select_add_fusion.2
  966.7 12.9 fusion.201
  987.0 13.5 fusion.203
  1095.2 46.2 %copy.269 = f32[392,392,16]{2,1,0:T(8,128)} copy(f32[392,392,16]{0,1,2:T(8,128)} %bitcast.176) | data formatting | bytes 19668992 | tf_op jit(solution)/shard_map/reshape | solution.py:349
  1141.5 820.1 %scatter_custom_fusion = f32[2535,16]{1,0:T(8,128)} fusion(s32[153664]{0:T(1024)} %reshape.431, f32[153664,16]{1,0:T(8,128)} %bitcast.23, f32[]{:T(128)} %constant.75.clone.1), kind=kCustom, calls=%fused_computation.129 | custom fusion | flops 2458624 | bytes 162752 | tf_op jit(solution)/shard_map/scatter-add | solution.py:348
  1976.0 34.9 %all-reduce.18 = (f32[512]{0:T(512)S(1)}, f32[512]{0:T(512)S(1)}, f32[512]{0:T(512)S(1)}, f32[2048]{0:T(1024)S(1)}, f32[512]{0:T(512)S(1)}, /*index=5*/f32[512]{...) all-reduce(f32[512]{0:T(512)S(1)} %convert_reduce_fusion.2, ...), channel_id=3, replica_groups=mesh['ta'=4,'ha'=2,'col'=4] {'ta','ha'}, use_global_device_ids=true, to_apply=%region_18.19.clone | all-reduce | flops 6144 | bytes 49152
  2020.3 80.3 %all-reduce.19 = (f32[64]{0:T(128)}, f32[64]{0:T(128)}, f32[64]{0:T(128)}, f32[256]{0:T(256)}, f32[64]{0:T(128)}, /*index=5*/f32[64]{0:T(128)}, f32[64]{0:T(128)...) all-reduce(f32[64]{0:T(128)S(1)} %dynamic-slice.9, ...), channel_id=1, replica_groups=mesh['ta'=4,'ha'=2,'col'=4] {'col'}, use_global_device_ids=true, to_apply=%region_19.20 | all-reduce | flops 5838 | bytes 46704 | tf_op jit(solution)/shard_map/psum | solution.py:386
  (449 shorter events, 413.7 us)
Async XLA Ops:
  7.2 536.9 %all-gather.6.cloned.1.call-start = ((), (), s32[]{:S(2)}) async-start(), calls=%async_computation.4 | async-start | bytes 1769472 | tf_op jit(solution)/shard_map/all_gather | solution.py:121
  23.3 642.5 %all-gather.8.cloned.1.call-start = ((), (), s32[]{:S(2)}) async-start(), calls=%async_computation.5 | async-start | bytes 2359296 | tf_op jit(solution)/shard_map/all_gather | solution.py:123
  38.6 661.3 %all-gather.10.cloned.1.call-start = ((), (), s32[]{:S(2)}) async-start(), calls=%async_computation.6 | async-start | bytes 2359296 | tf_op jit(solution)/shard_map/all_gather | solution.py:124
  41.6 20.5 copy-start.26
  42.8 397.1 %collective-permute-start = (bf16[2,4,7,14,512]{4,3,2,1,0:T(8,128)(2,1)}, bf16[2,4,7,14,512]{4,3,2,1,0:T(8,128)(2,1)}, u32[]{:S(2)}, u32[]{:S(2)}) collective-permute-start(bf16[2,4,7,14,512]{4,3,2,1,0:T(8,128)(2,1)} %copy.275), channel_id=1, source_target_pairs={{0,24},{8,0},{16,8},{24,16},{1,25},{9,1},{17,9},{25,17},{2,26},{10... | collective-permute-start | bytes 2408456 | tf_op jit(solution)/shard_map/ppermute | solution.py:22
  45.4 466.6 %collective-permute-start.4 = (bf16[2,4,7,14,512]{4,3,2,1,0:T(8,128)(2,1)}, bf16[2,4,7,14,512]{4,3,2,1,0:T(8,128)(2,1)}, u32[]{:S(2)}, u32[]{:S(2)}) collective-permute-start(bf16[2,4,7,14,512]{4,3,2,1,0:T(8,128)(2,1)} %copy.277), channel_id=1, source_target_pairs={{0,24},{8,0},{16,8},{24,16},{1,25},{9,1},{17,9},{25,17},{2,26},{10... | collective-permute-start | bytes 2408456 | tf_op jit(solution)/shard_map/ppermute | solution.py:22
  62.1 24.5 %copy-start.41 = (bf16[2535,2]{0,1:T(2,128)(2,1)S(1)}, bf16[2535,2]{0,1:T(2,128)(2,1)}, u32[]{:S(2)}) copy-start(bf16[2535,2]{0,1:T(2,128)(2,1)} %param.35) | copy-start | bytes 30424
  62.1 1904.3 %reduce-scatter.8.cloned.1.call-start = ((), (), s32[]{:S(2)}) async-start(), calls=%async_computation.8 | async-start | bytes 1179648 | tf_op jit(solution)/shard_map/reduce_scatter | solution.py:374
  384.9 54.6 %copy-start.60 = (s32[2,7]{1,0:T(2,128)S(1)}, s32[2,7]{1,0:T(2,128)}, u32[]{:S(2)}) copy-start(s32[2,7]{1,0:T(2,128)} %fusion.81) | copy-start | bytes 172
  384.9 54.8 %copy-start.40 = (s32[8,7]{1,0:T(8,128)S(1)}, s32[8,7]{1,0:T(8,128)}, u32[]{:S(2)}) copy-start(s32[8,7]{1,0:T(8,128)} %broadcast_add_fusion.1) | copy-start | bytes 676
  384.9 55.0 %copy-start.25 = (bf16[2,8,7,14,512]{4,3,2,1,0:T(8,128)(2,1)S(1)}, bf16[2,8,7,14,512]{4,3,2,1,0:T(8,128)(2,1)}, u32[]{:S(2)}) copy-start(bf16[2,8,7,14,512]{4,3,2,1,0:T(8,128)(2,1)} %copy_dynamic-update-slice_fusion.1) | copy-start | bytes 4816900
  439.5 30.0 %copy-start.63 = (bf16[512]{0:T(512)(128)(2,1)S(1)}, bf16[512]{0:T(512)(128)(2,1)}, u32[]{:S(2)}) copy-start(bf16[512]{0:T(512)(128)(2,1)} %get-tuple-element.425) | copy-start | bytes 3076
  439.5 30.6 %copy-start.62 = (bf16[512]{0:T(512)(128)(2,1)S(1)}, bf16[512]{0:T(512)(128)(2,1)}, u32[]{:S(2)}) copy-start(bf16[512]{0:T(512)(128)(2,1)} %get-tuple-element.426) | copy-start | bytes 3076
  439.5 31.2 %copy-start.39 = (bf16[128,64]{0,1:T(8,128)(2,1)S(1)}, bf16[128,64]{0,1:T(8,128)(2,1)}, u32[]{:S(2)}) copy-start(bf16[128,64]{0,1:T(8,128)(2,1)} %param.25) | copy-start | bytes 49156
  439.5 72.2 %copy-start.27 = (bf16[2,4,7,14,512]{4,1,3,2,0:T(4,128)(2,1)S(1)}, bf16[2,4,7,14,512]{4,1,3,2,0:T(4,128)(2,1)}, u32[]{:S(2)}) copy-start(bf16[2,4,7,14,512]{4,1,3,2,0:T(4,128)(2,1)} %get-tuple-element.443) | copy-start | bytes 2408452
  442.5 74.6 %collective-permute-start.1 = (bf16[2,8,3,14,512]{4,1,3,2,0:T(8,128)(2,1)}, bf16[2,8,3,14,512]{4,1,3,2,0:T(8,128)(2,1)}, u32[]{:S(2)}, u32[]{:S(2)}) collective-permute-start(bf16[2,8,3,14,512]{4,1,3,2,0:T(8,128)(2,1)} %copy.218), channel_id=1, source_target_pairs={{0,4},{4,0},{1,5},{5,1},{2,6},{6,2},{3,7},{7,3},{8,12},{12,8},{9,1... | collective-permute-start | bytes 2064392 | tf_op jit(solution)/shard_map/ppermute | solution.py:22
  515.6 17.8 collective-permute-start.5
  526.8 17.3 copy-start.35
  529.1 15.0 copy-start.37
  665.0 52.0 %copy-start.1 = (f32[1568,512]{1,0:T(8,128)}, f32[1568,512]{1,0:T(8,128)S(1)}, u32[]{:S(2)}) copy-start(f32[1568,512]{1,0:T(8,128)S(1)} %get-tuple-element.449) | copy-start | bytes 9633796
  665.1 51.9 %copy-start.30 = (f32[1568]{0:T(1024)}, f32[1568]{0:T(1024)S(1)}, u32[]{:S(2)}) copy-start(f32[1568]{0:T(1024)S(1)} %broadcast_multiply_fusion.4) | copy-start | bytes 18820
  665.8 51.3 %copy-start.33 = (f32[1568]{0:T(1024)}, f32[1568]{0:T(1024)S(1)}, u32[]{:S(2)}) copy-start(f32[1568]{0:T(1024)S(1)} %add_rsqrt_fusion) | copy-start | bytes 18820
  1027.3 939.1 %reduce-scatter.6.cloned.1.call-start = ((), (), s32[]{:S(2)}) async-start(), calls=%async_computation.7 | async-start | bytes 3538944 | tf_op jit(solution)/shard_map/reduce_scatter | solution.py:371
  1037.4 929.0 %reduce-scatter.10.cloned.1.call-start = ((), (), s32[]{:S(2)}) async-start(), calls=%async_computation.9 | async-start | bytes 4718592 | tf_op jit(solution)/shard_map/reduce_scatter | solution.py:376
  1046.7 919.7 %reduce-scatter.12.cloned.1.call-start = ((), (), s32[]{:S(2)}) async-start(), calls=%async_computation.10 | async-start | bytes 4718592 | tf_op jit(solution)/shard_map/reduce_scatter | solution.py:378
  1056.1 962.5 %all-reduce.25.cloned.1.call-start = ((), (), s32[]{:S(2)}) async-start(), calls=%async_computation.11 | async-start | bytes 2596864
  1074.1 889.1 %collective-permute-start.2 = (bf16[2,8,3,14,512]{4,1,3,2,0:T(8,128)(2,1)}, bf16[2,8,3,14,512]{4,1,3,2,0:T(8,128)(2,1)}, u32[]{:S(2)}, u32[]{:S(2)}) collective-permute-start(bf16[2,8,3,14,512]{4,1,3,2,0:T(8,128)(2,1)} %copy.237), channel_id=1, source_target_pairs={{0,4},{4,0},{1,5},{5,1},{2,6},{6,2},{3,7},{7,3},{8,12},{12,8},{9,1... | collective-permute-start | bytes 2064392 | tf_op jit(solution)/shard_map/ppermute | solution.py:22
  1093.9 875.8 %collective-permute-start.6 = (bf16[2,8,3,14,512]{4,1,3,2,0:T(8,128)(2,1)}, bf16[2,8,3,14,512]{4,1,3,2,0:T(8,128)(2,1)}, u32[]{:S(2)}, u32[]{:S(2)}) collective-permute-start(bf16[2,8,3,14,512]{4,1,3,2,0:T(8,128)(2,1)} %copy.256), channel_id=1, source_target_pairs={{0,4},{4,0},{1,5},{5,1},{2,6},{6,2},{3,7},{7,3},{8,12},{12,8},{9,1... | collective-permute-start | bytes 2064392 | tf_op jit(solution)/shard_map/ppermute | solution.py:22
  1141.5 820.4 %copy-start.13 = (bf16[2,2,8,7,7,512]{5,1,0,4,3,2:T(2,128)(2,1)S(1)}, bf16[2,2,8,7,7,512]{5,1,0,4,3,2:T(2,128)(2,1)}, u32[]{:S(2)}) copy-start(bf16[2,2,8,7,7,512]{5,1,0,4,3,2:T(2,128)(2,1)} %copy-done.12) | copy-start | bytes 4816900
  1961.6 158.5 %all-reduce.27.cloned.1.call-start = ((), (), s32[]{:S(2)}) async-start(), calls=%async_computation.12 | async-start | bytes 3145728 | tf_op jit(solution)/shard_map/psum | solution.py:386
  1969.8 131.9 %collective-permute-start.3 = (bf16[2,4,7,14,512]{4,1,3,2,0:T(4,128)(2,1)}, bf16[2,4,7,14,512]{4,1,3,2,0:T(4,128)(2,1)}, u32[]{:S(2)}, u32[]{:S(2)}) collective-permute-start(bf16[2,4,7,14,512]{4,1,3,2,0:T(4,128)(2,1)} %copy.239), channel_id=1, source_target_pairs={{0,8},{8,16},{16,24},{24,0},{1,9},{9,17},{17,25},{25,1},{2,10},{10... | collective-permute-start | bytes 2408456 | tf_op jit(solution)/shard_map/ppermute | solution.py:22
  1973.7 131.7 %collective-permute-start.7 = (bf16[2,4,7,14,512]{4,1,3,2,0:T(4,128)(2,1)}, bf16[2,4,7,14,512]{4,1,3,2,0:T(4,128)(2,1)}, u32[]{:S(2)}, u32[]{:S(2)}) collective-permute-start(bf16[2,4,7,14,512]{4,1,3,2,0:T(4,128)(2,1)} %copy.258), channel_id=1, source_target_pairs={{0,8},{8,16},{16,24},{24,0},{1,9},{9,17},{17,25},{25,1},{2,10},{10... | collective-permute-start | bytes 2408456 | tf_op jit(solution)/shard_map/ppermute | solution.py:22
  (62 other events, 257.9 us)
Sparse Core Ops, SparseCore 0:
  23.4 24.6 all-gather.5
  50.0 31.2 all-gather.7
  83.2 28.3 all-gather.9
  1027.4 33.7 reduce-scatter.7
  1064.5 54.6 reduce-scatter.5
  1122.8 50.2 reduce-scatter.9
  1176.4 51.3 reduce-scatter.11
  1961.7 56.8 all-reduce.24
  2021.2 98.8 all-reduce.26
where the time goes:
time: 2150 us; the launch traced here: 2130 us
  other arithmetic  866 us (40%)
  local copies, waits for them, and re-layouts  588 us (27%)
  matrix products  375 us (17%)
  blocking collectives  258 us (12%)
    scatter-add x1, other arithmetic, per_device(): jax.ops.segment_sum(table_terms.transpose(1, 2, 0).reshape(WIN * WIN, HEA...  820 us
    gather x2, local copies, waits for them, and re-layouts, per_device(): position_bias = table_full[rel_index].transpose(2, 0, 1)  337 us
    psum x1, blocking collectives, per_device(): lax.psum((shares[0], shares[1], shares[2], shares[3], shares[4], shares[5...  80.3 us
    sub x4, matrix products, attend_backward(): grad_prob - jnp.sum(probability * grad_prob, axis=-1, keepdims=True)  70.1 us
    dot_general x8, matrix products, window_scores(): jnp.einsum('qhd,khd->hqk', query_head, key_head, preferred_element_type=j...  63 us
    dot_general x4, matrix products, attend_backward(): jnp.einsum('hqk,qhd->khd', scaled, query_head, preferred_element_type=jnp...  53.9 us
    dot_general x4, matrix products, attend_backward(): jnp.einsum('hqk,khd->qhd', scaled, key_head, preferred_element_type=jnp.f...  51.7 us
    unnamed x2, blocking collectives  49.7 us
  transfers between devices with their start and end apart: 17, of which 3 were waited for; matrix products, arithmetic and copies ran while one was open for 70% of the time, Pallas kernels for 0%

commit v1 on v0

v1 whole, which is shorter than its diff:
```python
import jax
import jax.numpy as jnp
import numpy as np
from jax import lax
from jax.experimental import pallas as pl
from jax.experimental.pallas import tpu as pltpu
from jax.sharding import PartitionSpec as P

D = 512
HEADS = 16
FF = 2048
WIN_T = 8
WIN_H = 7
WIN_W = 7
HEAD_DIM = 32
SHIFT_T = 4
SHIFT_H = 3
SHIFT_W = 3
WIDTH = 14
WIN = 392
RPB_ROWS = 2535

ROWS = 400
LANES = 128
GROUP = LANES // HEAD_DIM
CELLS = WIN_H * WIN_W
CELL_ROWS = 56
CELL_LANES = 64
DIFF_T = 2 * WIN_T - 1
DIFF_HW = (2 * WIN_H - 1) * (2 * WIN_W - 1)
SPAN = WIN_T * CELL_LANES
WIDE = 2 * SPAN
LOG2E = 1.4426950408889634
SCALE = HEAD_DIM**-0.5

f32 = jnp.float32
bf16 = jnp.bfloat16
NN = (((1,), (0,)), ((), ()))
NT = (((1,), (1,)), ((), ()))
TN = (((0,), (0,)), ((), ()))


def mm(left, right, dims):
    return lax.dot_general(left, right, dims, preferred_element_type=f32)


def flipped(value, axis, bit):
    devices = lax.axis_size(axis)
    return lax.ppermute(value, axis, [(i, i ^ bit) for i in range(devices)])


def bits_of(axis):
    count = lax.axis_size(axis)
    assert count & (count - 1) == 0
    return [1 << n for n in range(count.bit_length() - 1)]


def both_orders(mine, theirs, axis, bit):
    high = (lax.axis_index(axis) & bit) != 0
    return jnp.stack([jnp.where(high, theirs, mine), jnp.where(high, mine, theirs)])


def doubled(value, steps):
    for axis, bit in steps:
        value = both_orders(value, flipped(value, axis, bit), axis, bit)
    return value


def tile_steps():
    ta_bits = bits_of("ta")
    return [("ta", b) for b in ta_bits[1:]] + [("ha", b) for b in bits_of("ha")] + [("ta", b) for b in ta_bits[:1]]


def ordered(value, steps, axes):
    got = list(reversed(steps))
    want = [(axis, b) for axis in axes for b in reversed(bits_of(axis))]
    lead = len(got)
    order = [got.index(w) for w in want]
    value = value.transpose(order + list(range(lead, value.ndim)))
    sizes = [lax.axis_size(axis) for axis in axes]
    return value.reshape(sizes + list(value.shape[lead:]))


def summed_share(value, low):
    ta_bits = bits_of("ta")
    ha_bits = bits_of("ha")
    names = [("ta", b) for b in reversed(ta_bits)] + [("ha", b) for b in reversed(ha_bits)]
    value = value.reshape((2,) * len(names) + value.shape[1:])
    for axis, bit in [("ta", b) for b in ta_bits[:1]] + [("ha", b) for b in ha_bits] + [("ta", b) for b in ta_bits[1:]]:
        at = names.index((axis, bit))
        high = jnp.where((lax.axis_index(axis) & bit) != 0, 1, 0)
        keep = lax.dynamic_index_in_dim(value, high, at, keepdims=False)
        send = lax.dynamic_index_in_dim(value, 1 - high, at, keepdims=False)
        if low:
            send = send.astype(bf16)
        value = keep + flipped(send, axis, bit).astype(f32)
        names.pop(at)
    return value


def summed_col(value, low):
    for bit in bits_of("col"):
        if low:
            value = value.astype(bf16)
        value = value.astype(f32) + flipped(value, "col", bit).astype(f32)
    return value


def rank_shifted(value, ta_by, ha_by):
    n_ta, n_ha = lax.axis_size("ta"), lax.axis_size("ha")
    pairs = [
        (t * n_ha + h, ((t + ta_by) % n_ta) * n_ha + (h + ha_by) % n_ha) for t in range(n_ta) for h in range(n_ha)
    ]
    return lax.ppermute(value, ("ta", "ha"), pairs)


def moved(piece, ta_by, ha_by):
    shape = piece.shape
    return rank_shifted(piece.reshape(-1, D), ta_by, ha_by).reshape(shape)


def windows_in(tile):
    clips = tile.shape[0]
    t, h = SHIFT_T, SHIFT_H
    own = tile[:, t:, h:]
    down = moved(tile[:, t:, :h], 0, -1)
    ahead = moved(tile[:, :t, h:], -1, 0)
    corner = moved(tile[:, :t, :h], -1, -1)
    grid = jnp.concatenate(
        [jnp.concatenate([own, down], axis=2), jnp.concatenate([ahead, corner], axis=2)], axis=1
    )
    left = grid[:, :, :, SHIFT_W : SHIFT_W + WIN_W]
    right = jnp.concatenate([grid[:, :, :, SHIFT_W + WIN_W :], grid[:, :, :, :SHIFT_W]], axis=3)
    rows = jnp.stack([left, right], axis=1).reshape(2 * clips, WIN, D)
    return jnp.pad(rows, ((0, 0), (0, ROWS - WIN), (0, 0)))


def windows_out(rows, clips):
    t, h = SHIFT_T, SHIFT_H
    grid = rows[:, :WIN].reshape(clips, 2, WIN_T, WIN_H, WIN_W, D)
    left, right = grid[:, 0], grid[:, 1]
    cut = WIN_W - SHIFT_W
    grid = jnp.concatenate([right[:, :, :, cut:], left, right[:, :, :, :cut]], axis=3)
    kind = rows.dtype
    down = moved(grid[:, :t, WIN_H - h :].astype(bf16), 0, 1).astype(kind)
    ahead = moved(grid[:, t:, : WIN_H - h].astype(bf16), 1, 0).astype(kind)
    corner = moved(grid[:, t:, WIN_H - h :].astype(bf16), 1, 1).astype(kind)
    own = grid[:, :t, : WIN_H - h]
    return jnp.concatenate(
        [jnp.concatenate([corner, ahead], axis=2), jnp.concatenate([down, own], axis=2)], axis=1
    )


def cell_one_hot():
    cell = np.arange(CELLS)
    r, c = cell // WIN_W, cell % WIN_W
    diff = (r[:, None] - r[None, :] + WIN_H - 1) * (2 * WIN_W - 1) + c[:, None] - c[None, :] + WIN_W - 1
    diff = np.pad(diff, ((0, 0), (0, CELL_LANES - CELLS)), constant_values=-1).reshape(-1)
    return jnp.asarray(diff, jnp.int32)[None, :] == lax.broadcasted_iota(jnp.int32, (DIFF_HW, diff.size), 0)


def packed_position(index):
    return index // CELLS, index % CELLS


def row_picker(rows_first):
    shape = (ROWS, WIN_T * CELL_ROWS) if rows_first else (WIN_T * CELL_ROWS, ROWS)
    i = lax.broadcasted_iota(jnp.int32, shape, 0 if rows_first else 1)
    p = lax.broadcasted_iota(jnp.int32, shape, 1 if rows_first else 0)
    frame, cell = packed_position(i)
    return jnp.where((p == frame * CELL_ROWS + cell) & (i < WIN), 1.0, 0.0).astype(bf16)


def lane_picker(padded_first):
    shape = (SPAN, ROWS) if padded_first else (ROWS, SPAN)
    j = lax.broadcasted_iota(jnp.int32, shape, 1 if padded_first else 0)
    p = lax.broadcasted_iota(jnp.int32, shape, 0 if padded_first else 1)
    frame, cell = packed_position(j)
    return jnp.where((p == frame * CELL_LANES + cell) & (j < WIN), 1.0, 0.0).astype(bf16)


def bias_kernel(cells_ref, rows_ref, lanes_ref, bias_ref):
    cells = cells_ref[0].astype(f32)
    frames = []
    for frame in range(WIN_T):
        start = (WIN_T - 1 - frame) * CELL_LANES
        frames.append(pltpu.roll(cells, (WIDE - start) % WIDE, 1)[:, :SPAN].astype(bf16))
    picked = jnp.zeros((ROWS, SPAN), f32)
    for frame in range(WIN_T):
        picked = picked + mm(rows_ref[frame], frames[frame], NN)
    bias_ref[0] = mm(picked.astype(bf16), lanes_ref[...], NN) * LOG2E


def expanded_bias(cells):
    rows = row_picker(True).reshape(ROWS, WIN_T, CELL_ROWS).transpose(1, 0, 2)
    return pl.pallas_call(
        bias_kernel,
        grid=(HEADS,),
        in_specs=[
            pl.BlockSpec((1, CELL_ROWS, WIDE), lambda h: (h, 0, 0)),
            pl.BlockSpec((WIN_T, ROWS, CELL_ROWS), lambda h: (0, 0, 0)),
            pl.BlockSpec((SPAN, ROWS), lambda h: (0, 0)),
        ],
        out_specs=pl.BlockSpec((1, ROWS, ROWS), lambda h: (h, 0, 0)),
        out_shape=jax.ShapeDtypeStruct((HEADS, ROWS, ROWS), f32),
        name="bias_expand",
    )(cells, rows, lane_picker(True))


def halves(value):
    high = value.astype(bf16)
    return high, (value - high.astype(f32)).astype(bf16)


def bias_grad_kernel(grad_ref, rows_ref, lanes_ref, cells_ref):
    total = jnp.zeros((CELL_ROWS, WIDE), f32)
    high, low = halves(grad_ref[0])
    spread = mm(high, lanes_ref[...], NN) + mm(low, lanes_ref[...], NN)
    high, low = halves(spread)
    for frame in range(WIN_T):
        picked = mm(rows_ref[frame], high, NN) + mm(rows_ref[frame], low, NN)
        picked = jnp.concatenate([picked, jnp.zeros((CELL_ROWS, SPAN), f32)], axis=1)
        total = total + pltpu.roll(picked, (WIN_T - 1 - frame) * CELL_LANES, 1)
    cells_ref[0] = total


def collected_bias_grad(grad):
    rows = row_picker(False).reshape(WIN_T, CELL_ROWS, ROWS)
    return pl.pallas_call(
        bias_grad_kernel,
        grid=(HEADS,),
        in_specs=[
            pl.BlockSpec((1, ROWS, ROWS), lambda h: (h, 0, 0)),
            pl.BlockSpec((WIN_T, CELL_ROWS, ROWS), lambda h: (0, 0, 0)),
            pl.BlockSpec((ROWS, SPAN), lambda h: (0, 0)),
        ],
        out_specs=pl.BlockSpec((1, CELL_ROWS, WIDE), lambda h: (h, 0, 0)),
        out_shape=jax.ShapeDtypeStruct((HEADS, CELL_ROWS, WIDE), f32),
        name="bias_collect",
    )(grad, rows, lane_picker(False))


def difference_rows(rel_index):
    dt = np.arange(DIFF_T)[::-1] - (WIN_T - 1)
    dr = np.arange(2 * WIN_H - 1) - (WIN_H - 1)
    dc = np.arange(2 * WIN_W - 1) - (WIN_W - 1)
    t, r, c = np.meshgrid(dt, dr, dc, indexing="ij")

    def place(sign):
        a, b, d = (np.maximum(sign * v, 0) for v in (t, r, c))
        return ((a * WIN_H + b) * WIN_W + d).reshape(-1)

    flat = place(1) * WIN + place(-1)
    return rel_index.reshape(-1)[jnp.asarray(flat, jnp.int32)]


def forward_kernel(q_ref, k_ref, v_ref, ask_ref, tell_ref, bias_ref, mix_ref, inv_ref, exp_ref):
    group = lax.broadcasted_iota(jnp.int32, (ROWS, LANES), 1) // HEAD_DIM
    q, k, v = q_ref[0], k_ref[0], v_ref[0]
    ask, tell = ask_ref[0], tell_ref[0]
    zero = jnp.zeros((ROWS, LANES), bf16)
    one = jnp.ones((ROWS, LANES), bf16)
    for h in range(GROUP):
        own = group == h
        spare = group == (h + 1) % GROUP
        q_h = jnp.where(own, q, jnp.where(spare, ask, zero))
        k_h = jnp.where(own, k, jnp.where(spare, tell, zero))
        v_h = jnp.where(own, v, one)
        scores = mm(q_h, k_h, NT) + bias_ref[h]
        exponent = jnp.exp2(scores - jnp.max(scores, axis=1, keepdims=True)).astype(bf16)
        exp_ref[0, h] = exponent
        mixed = mm(exponent, v_h, NN)
        inverse = 1.0 / pltpu.roll(mixed, HEAD_DIM, 1)
        mixture = (mixed * inverse).astype(bf16)
        if h == 0:
            mix_ref[0] = mixture
            inv_ref[0] = inverse
        else:
            mix_ref[0] = jnp.where(own, mixture, mix_ref[0])
            inv_ref[0] = jnp.where(own, inverse, inv_ref[0])


def head_block(offset):
    return pl.BlockSpec((1, ROWS, LANES), lambda g, w: (w, 0, g + offset))


def attention_forward(qkv, ask, tell, bias):
    wins = qkv.shape[0]
    per_group = D // LANES
    pair = pl.BlockSpec((1, ROWS, LANES), lambda g, w: (w, 0, 0))
    return pl.pallas_call(
        forward_kernel,
        grid=(per_group, wins),
        in_specs=[
            head_block(0),
            head_block(per_group),
            head_block(2 * per_group),
            pair,
            pair,
            pl.BlockSpec((GROUP, ROWS, ROWS), lambda g, w: (g, 0, 0)),
        ],
        out_specs=[
            head_block(0),
            head_block(0),
            pl.BlockSpec((1, GROUP, ROWS, ROWS), lambda g, w: (w, g, 0, 0)),
        ],
        out_shape=[
            jax.ShapeDtypeStruct((wins, ROWS, D), bf16),
            jax.ShapeDtypeStruct((wins, ROWS, D), f32),
            jax.ShapeDtypeStruct((wins, HEADS, ROWS, ROWS), bf16),
        ],
        name="attention_forward",
    )(qkv, qkv, qkv, ask, tell, bias)


def backward_kernel(
    q_ref, k_ref, v_ref, mix_ref, inv_ref, exp_ref, grad_ref, dq_ref, dk_ref, dv_ref, bias_ref
):
    win = pl.program_id(1)
    lane = lax.broadcasted_iota(jnp.int32, (ROWS, LANES), 1)
    group, within = lane // HEAD_DIM, lane % HEAD_DIM
    q, k, v = q_ref[0], k_ref[0], v_ref[0]
    inverse = inv_ref[0]
    grad = grad_ref[0].astype(f32)
    side_a = lax.broadcasted_iota(jnp.int32, (LANES, LANES), 0) // HEAD_DIM
    side_b = lax.broadcasted_iota(jnp.int32, (LANES, LANES), 1) // HEAD_DIM
    same = jnp.where(side_a == side_b, 1.0, 0.0).astype(bf16)
    high, low = halves(grad * mix_ref[0].astype(f32))
    drop = pltpu.roll((mm(high, same, NN) + mm(low, same, NN)) * inverse, HEAD_DIM, 1)
    high, low = halves(-drop)
    zero = jnp.zeros((ROWS, LANES), bf16)
    ask = jnp.where(within == 0, high, jnp.where(within == 1, low, zero))
    tell = jnp.where(within < 2, jnp.ones((ROWS, LANES), bf16), zero)
    scaled = (grad * inverse).astype(bf16)
    for h in range(GROUP):
        own = group == h
        spare = group == (h + 1) % GROUP
        grad_h = jnp.where(own, scaled, jnp.where(spare, ask, zero))
        v_h = jnp.where(own, v, jnp.where(spare, tell, zero))
        exponent = exp_ref[0, h]
        grad_scores = exponent.astype(f32) * mm(grad_h, v_h, NT)

        @pl.when(win == 0)
        def _():
            bias_ref[h] = grad_scores

        @pl.when(win != 0)
        def _():
            bias_ref[h] += grad_scores

        low_scores = grad_scores.astype(bf16)
        dq = (mm(low_scores, k, NN) * SCALE).astype(bf16)
        dk = (mm(low_scores, q, TN) * (1.0 / LOG2E)).astype(bf16)
        dv = mm(exponent, scaled, TN).astype(bf16)
        if h == 0:
            dq_ref[0], dk_ref[0], dv_ref[0] = dq, dk, dv
        else:
            dq_ref[0] = jnp.where(own, dq, dq_ref[0])
            dk_ref[0] = jnp.where(own, dk, dk_ref[0])
            dv_ref[0] = jnp.where(own, dv, dv_ref[0])


def attention_backward(qkv, mixture, inverse, exponent, grad):
    wins = qkv.shape[0]
    per_group = D // LANES
    return pl.pallas_call(
        backward_kernel,
        grid=(per_group, wins),
        in_specs=[
            head_block(0),
            head_block(per_group),
            head_block(2 * per_group),
            head_block(0),
            head_block(0),
            pl.BlockSpec((1, GROUP, ROWS, ROWS), lambda g, w: (w, g, 0, 0)),
            head_block(0),
        ],
        out_specs=[head_block(0)] * 3 + [pl.BlockSpec((GROUP, ROWS, ROWS), lambda g, w: (g, 0, 0))],
        out_shape=[jax.ShapeDtypeStruct((wins, ROWS, D), bf16)] * 3
        + [jax.ShapeDtypeStruct((HEADS, ROWS, ROWS), f32)],
        name="attention_backward",
    )(qkv, qkv, qkv, mixture, inverse, exponent, grad)


def mask_pairs(clips):
    index = np.arange(ROWS)
    frame, cell = packed_position(index)
    late_t = jnp.asarray((frame >= WIN_T - SHIFT_T).astype(np.int32))
    late_r = jnp.asarray((cell // WIN_W >= WIN_H - SHIFT_H).astype(np.int32))
    late_c = jnp.asarray((cell % WIN_W >= WIN_W - SHIFT_W).astype(np.int32))
    last_t = (lax.axis_index("ta") == lax.axis_size("ta") - 1).astype(jnp.int32)
    last_r = (lax.axis_index("ha") == lax.axis_size("ha") - 1).astype(jnp.int32)
    base = late_t * last_t * 4 + late_r * last_r * 2
    region = jnp.stack([base, base + late_c])[:, :, None]
    lane = lax.broadcasted_iota(jnp.int32, (2, ROWS, LANES), 2) % HEAD_DIM
    real = lax.broadcasted_iota(jnp.int32, (2, ROWS, LANES), 1) < WIN
    full = np.float32(-100.0 * LOG2E)
    high = np.float32(full.astype(jnp.bfloat16))
    rest = np.float32(np.float64(-100.0 * LOG2E) - np.float64(high))
    ask = jnp.where(lane < 16, (lane % 8 == region).astype(f32), (lane == 16).astype(f32))
    apart = (lane % 8 != region) & real
    tell = jnp.where(
        lane < 8,
        jnp.where(apart, high, 0.0),
        jnp.where(lane < 16, jnp.where(apart, rest, 0.0), jnp.where((lane == 16) & ~real, -1e30, 0.0)),
    )
    return jnp.tile(ask.astype(bf16), (clips, 1, 1)), jnp.tile(tell.astype(bf16), (clips, 1, 1))


def norm_rows(values, norm_gain, norm_shift):
    centre = values - jnp.mean(values, axis=-1, keepdims=True)
    inv_std = lax.rsqrt(jnp.mean(centre * centre, axis=-1, keepdims=True) + 1e-05)
    normed = centre * inv_std
    return (normed, inv_std, normed * norm_gain + norm_shift)


def norm_back(grad_out, normed, inv_std, norm_gain):
    scaled = grad_out * norm_gain
    return inv_std * (
        scaled
        - jnp.mean(scaled, axis=-1, keepdims=True)
        - normed * jnp.mean(scaled * normed, axis=-1, keepdims=True)
    )


def gelu_slope(values):
    normal_cdf = 0.5 * (1.0 + lax.erf(values * 0.7071067811865476))
    return normal_cdf + values * jnp.exp(-0.5 * values * values) * 0.3989422804014327


def per_device(
    tokens,
    qkv_weight,
    query_bias,
    value_bias,
    proj_weight,
    proj_bias,
    fc1_weight,
    fc1_bias,
    fc2_weight,
    fc2_bias,
    norm1_gain,
    norm1_shift,
    norm2_gain,
    norm2_shift,
    bias_table,
    rel_index,
    cotangent,
):
    clips = tokens.shape[0]
    n_col = lax.axis_size("col")
    tiles = lax.axis_size("ta") * lax.axis_size("ha")
    steps = tile_steps()

    vectors = [
        query_bias,
        value_bias,
        proj_bias,
        fc1_bias,
        fc2_bias,
        norm1_gain,
        norm1_shift,
        norm2_gain,
        norm2_shift,
    ]
    heads_here = bias_table.shape[1]
    sizes = [v.shape[0] for v in vectors] + [RPB_ROWS * heads_here]
    small = jnp.concatenate(vectors + [bias_table.T.reshape(-1)])
    small_len = -(-small.shape[0] // LANES) * LANES
    small = jnp.pad(small, (0, small_len - small.shape[0])).reshape(-1, LANES)
    small_full = ordered(doubled(small, steps), steps, ("ta", "ha")).reshape(tiles, -1).astype(f32)
    cuts = np.cumsum([0] + sizes)
    parts = [small_full[:, a:b] for a, b in zip(cuts[:-1], cuts[1:])]
    (
        bias_query,
        bias_value,
        bias_proj,
        bias_fc1,
        bias_fc2,
        gain_one,
        shift_one,
        gain_two,
        shift_two,
    ) = [p.reshape(-1) for p in parts[:-1]]
    table = parts[-1].reshape(HEADS, RPB_ROWS)

    col_steps = [("col", b) for b in bits_of("col")]
    qkv_steps = col_steps + steps
    qkv_full = ordered(doubled(qkv_weight, qkv_steps), qkv_steps, ("col", "ta", "ha"))
    qkv_full = qkv_full.transpose(0, 3, 1, 2, 4).reshape(D, 3 * D)

    x_rows = windows_in(tokens).reshape(-1, D).astype(f32)
    wins = 2 * clips

    later = jnp.concatenate(
        [proj_weight.reshape(-1, LANES), fc1_weight.reshape(-1, LANES), fc2_weight.reshape(-1, LANES)]
    )
    later = lax.all_gather(later, ("col", "ta", "ha"), axis=0).reshape(n_col, tiles, -1, LANES)
    cuts = np.cumsum([0, proj_weight.size // LANES, fc1_weight.size // LANES, fc2_weight.size // LANES])

    def whole(at, shape):
        piece = later[:, :, cuts[at] : cuts[at + 1]].reshape((n_col, tiles) + shape)
        return piece.transpose(0, 2, 1, 3).reshape(n_col * shape[0], tiles * shape[1])

    proj_full = whole(0, proj_weight.shape)
    fc1_full = whole(1, fc1_weight.shape)
    fc2_full = whole(2, fc2_weight.shape)

    grad_out = windows_in(cotangent).reshape(-1, D)

    table_rows = difference_rows(rel_index)
    by_difference = jnp.take(table, table_rows, axis=1).astype(bf16).reshape(HEADS * DIFF_T, DIFF_HW)
    one_hot = cell_one_hot().astype(bf16)
    cells = mm(by_difference, one_hot, NN).astype(bf16)
    cells = cells.reshape(HEADS, DIFF_T, CELLS, CELL_LANES).transpose(0, 2, 1, 3)
    cells = jnp.pad(cells, ((0, 0), (0, CELL_ROWS - CELLS), (0, 1), (0, 0))).reshape(HEADS, CELL_ROWS, WIDE)
    position_bias = expanded_bias(cells)
    ask, tell = mask_pairs(clips)

    normed_one, inv_one, pre_one = norm_rows(x_rows, gain_one, shift_one)
    entry_rows = pre_one.astype(bf16)
    projected = jnp.dot(entry_rows, qkv_full, preferred_element_type=f32)
    offsets = jnp.concatenate([bias_query, jnp.zeros((D,), f32), bias_value])
    scales = jnp.concatenate([jnp.full((D,), SCALE * LOG2E, f32), jnp.ones((2 * D,), f32)])
    qkv = ((projected + offsets) * scales).astype(bf16).reshape(wins, ROWS, 3 * D)
    mixture, inverse, exponent = attention_forward(qkv, ask, tell, position_bias)
    mixture_rows = mixture.reshape(-1, D)
    middle = x_rows + (jnp.dot(mixture_rows, proj_full, preferred_element_type=f32) + bias_proj)
    normed_two, inv_two, pre_two = norm_rows(middle, gain_two, shift_two)
    second = pre_two.astype(bf16)
    hidden = jnp.dot(second, fc1_full, preferred_element_type=f32) + bias_fc1
    activation = jax.nn.gelu(hidden, approximate=False).astype(bf16)
    result = middle + (jnp.dot(activation, fc2_full, preferred_element_type=f32) + bias_fc2)
    block_out = windows_out(result.astype(bf16).reshape(wins, ROWS, D), clips)

    grad_fc2_bias = jnp.sum(grad_out.astype(f32), axis=0)
    grad_fc2_t = mm(grad_out, activation, TN)
    grad_act = mm(grad_out, fc2_full, NT)
    grad_hidden = grad_act * gelu_slope(hidden)
    grad_fc1_bias = jnp.sum(grad_hidden, axis=0)
    hidden_low = grad_hidden.astype(bf16)
    grad_fc1_t = mm(hidden_low, second, TN)
    grad_second = mm(hidden_low, fc1_full, NT)
    grad_gain_two = jnp.sum(grad_second * normed_two, axis=0)
    grad_shift_two = jnp.sum(grad_second, axis=0)
    grad_middle = grad_out.astype(f32) + norm_back(grad_second, normed_two, inv_two, gain_two)
    grad_proj_bias = jnp.sum(grad_middle, axis=0)
    middle_low = grad_middle.astype(bf16)
    grad_proj_t = mm(middle_low, mixture_rows, TN)
    grad_mixture = mm(middle_low, proj_full, NT).astype(bf16)

    early = jnp.concatenate(
        [
            grad_proj_t.astype(bf16).reshape(tiles, -1, D),
            grad_fc1_t.astype(bf16).reshape(tiles, -1, D),
            grad_fc2_t.astype(bf16).reshape(tiles, -1, D),
        ],
        axis=1,
    )
    early = lax.psum(lax.psum_scatter(early, ("ta", "ha"), scatter_dimension=0), "col").astype(f32)
    cuts = np.cumsum([0, D // tiles, FF // tiles, FF // tiles])
    share_proj = early[cuts[0] : cuts[1]].T
    share_fc1 = early[cuts[1] : cuts[2]].T
    share_fc2 = early[cuts[2] : cuts[3]].reshape(D // tiles, FF).T

    grad_q, grad_k, grad_v, bias_pairs = attention_backward(
        qkv, mixture, inverse, exponent, grad_mixture.reshape(wins, ROWS, D)
    )
    grad_queries, grad_keys, grad_values = [g.reshape(-1, D) for g in (grad_q, grad_k, grad_v)]
    grad_query_bias = jnp.sum(grad_queries.astype(f32), axis=0)
    grad_value_bias = jnp.sum(grad_values.astype(f32), axis=0)
    grad_qkv_t = jnp.concatenate([mm(g, entry_rows, TN) for g in (grad_queries, grad_keys, grad_values)])
    share_qkv = summed_col(summed_share(grad_qkv_t.reshape(tiles, -1, D), True), True).T

    cell_grads = collected_bias_grad(bias_pairs)[:, :CELLS, : DIFF_T * CELL_LANES]
    cell_grads = cell_grads.reshape(HEADS, CELLS, DIFF_T, CELL_LANES).transpose(0, 2, 1, 3)
    by_difference = lax.dot_general(
        cell_grads.reshape(HEADS * DIFF_T, CELLS * CELL_LANES),
        cell_one_hot().astype(f32),
        NT,
        precision=lax.Precision.HIGHEST,
        preferred_element_type=f32,
    ).reshape(HEADS, RPB_ROWS)

    grad_entry = (
        mm(grad_queries, qkv_full[:, :D], NT)
        + mm(grad_keys, qkv_full[:, D : 2 * D], NT)
        + mm(grad_values, qkv_full[:, 2 * D :], NT)
    )
    grad_gain_one = jnp.sum(grad_entry * normed_one, axis=0)
    grad_shift_one = jnp.sum(grad_entry, axis=0)
    grad_tokens = grad_middle + norm_back(grad_entry, normed_one, inv_one, gain_one)
    tokens_grad = windows_out(grad_tokens.reshape(wins, ROWS, D), clips)

    pieces = [
        grad_query_bias,
        grad_value_bias,
        grad_proj_bias,
        grad_fc1_bias,
        grad_fc2_bias,
        grad_gain_one,
        grad_shift_one,
        grad_gain_two,
        grad_shift_two,
        by_difference,
    ]
    flat = jnp.concatenate([p.reshape(tiles, -1) for p in pieces], axis=1)
    flat = jnp.pad(flat, ((0, 0), (0, small_len - flat.shape[1]))).reshape(tiles, -1, LANES)
    shares = summed_col(summed_share(flat, False), False).reshape(-1)
    cuts = np.cumsum([0] + sizes)
    outs = [shares[a:b] for a, b in zip(cuts[:-1], cuts[1:])]
    places = jnp.zeros((RPB_ROWS,), jnp.int32).at[table_rows].set(jnp.arange(RPB_ROWS, dtype=jnp.int32))
    share_table = jnp.take(outs[-1].reshape(heads_here, RPB_ROWS), places, axis=1).T

    return (
        block_out,
        tokens_grad,
        share_qkv,
        outs[0],
        outs[1],
        share_proj,
        outs[2],
        share_fc1,
        outs[3],
        share_fc2,
        outs[4],
        outs[5],
        outs[6],
        outs[7],
        outs[8],
        share_table,
    )


def solution(mesh):
    tile = P("col", "ta", "ha", None, None)
    weight = P("col", ("ta", "ha"))
    vector = P(("ta", "ha"))
    share = P(None, ("ta", "ha"))
    return jax.shard_map(
        per_device,
        mesh=mesh,
        in_specs=(
            tile,
            weight,
            vector,
            vector,
            weight,
            vector,
            weight,
            vector,
            weight,
            vector,
            vector,
            vector,
            vector,
            vector,
            share,
            P(),
            tile,
        ),
        out_specs=(
            tile,
            tile,
            share,
            vector,
            vector,
            share,
            vector,
            share,
            vector,
            share,
            vector,
            vector,
            vector,
            vector,
            vector,
            share,
        ),
        check_vma=False,
    )
```

time: 2150 us -> 651 us (0.30)
  other arithmetic: 866 us -> 58.2 us
  local copies, waits for them, and re-layouts: 588 us -> 237 us
  matrix products: 375 us -> 97.6 us
  blocking collectives: 258 us -> 0 us
  Pallas kernels: 0 us -> 147 us
  waiting for transfers between devices: 19.8 us -> 56.4 us
    scatter-add x1 -> x0, other arithmetic: 820 us -> none  [per_device(): jax.ops.segment_sum(table_terms.transpose(1, 2, 0).reshape(WIN * WIN, HEA...]
    gather x2 -> x6, local copies, waits for them, and re-layouts: 337 us -> 26.9 us  [the longest x2 13.7 us: difference_rows(): return rel_index.reshape(-1)[jnp.asarray(flat, jnp.int32)]]
    dot_general x36 -> x18, matrix products: 305 us -> 97.6 us  [the longest x13 48.8 us: mm(): return lax.dot_general(left, right, dims, preferred_element_type=f32)]
    pallas_call x0 -> x4, Pallas kernels: none -> 147 us  [the longest x1 57.5 us: attention_backward(): pl.pallas_call(backward_kernel, grid=(per_group, wins), in_specs=[head_bl...]
    all_gather x7 -> x0, blocking collectives: 128 us -> none  [the longest x1 28.9 us: gather_weights(): lax.all_gather(col_whole[1], ('ta', 'ha'), axis=1, tiled=True)]
    psum x1 -> x0, blocking collectives: 80.3 us -> none  [per_device(): lax.psum((shares[0], shares[1], shares[2], shares[3], shares[4], shares[5...]
    sub x4 -> x0, matrix products: 70.1 us -> none  [attend_backward(): grad_prob - jnp.sum(probability * grad_prob, axis=-1, keepdims=True)]
    unnamed x2 -> x0, blocking collectives: 49.7 us -> none
  transfers between devices with their start and end apart: 17 -> 33, of which waited for: 3 -> 9; matrix products, arithmetic and copies ran while one was open for 70% -> 35% of each run, Pallas kernels for 0% -> 14%
where the time goes in v1:
time: 651 us; the launch traced here: 641 us
  local copies, waits for them, and re-layouts  237 us (36%)
  Pallas kernels  147 us (23%)
  matrix products  97.6 us (15%)
  other arithmetic  58.2 us (9%)
  waiting for transfers between devices  56.4 us (9%)
  starting transfers between devices  28.9 us (4%)
  between operations  15.8 us (2%)
    pallas_call x1, Pallas kernels, attention_backward(): pl.pallas_call(backward_kernel, grid=(per_group, wins), in_specs=[head_bl...  57.5 us
    dot_general x13, matrix products, mm(): return lax.dot_general(left, right, dims, preferred_element_type=f32)  48.8 us
    pallas_call x1, Pallas kernels, attention_forward(): pl.pallas_call(forward_kernel, grid=(per_group, wins), in_specs=[head_blo...  34.9 us
    dot_general x1, matrix products, per_device(): hidden = jnp.dot(second, fc1_full, preferred_element_type=f32) + bias_fc1  34 us
    ppermute x18, waiting for transfers between devices, flipped(): return lax.ppermute(value, axis, [(i, i ^ bit) for i in range(devices)])  33.5 us
    pallas_call x1, Pallas kernels, collected_bias_grad(): pl.pallas_call(bias_grad_kernel, grid=(HEADS,), in_specs=[pl.BlockSpec((1...  32.2 us
    reshape x24, local copies, waits for them, and re-layouts, moved(): return rank_shifted(piece.reshape(-1, D), ta_by, ha_by).reshape(shape)  28.8 us
    unnamed x163, local copies, waits for them, and re-layouts  25 us
  transfers between devices with their start and end apart: 33, of which 9 were waited for; matrix products, arithmetic and copies ran while one was open for 35% of the time, Pallas kernels for 14%

profile of v1, /device:TPU:0, one launch (start us, length us, event | category | flops | bytes accessed | tf_op | source)
XLA Modules:
  0.0 641.2 jit_solution(6621032211875678512)
XLA Ops:
  8.0 6.1 concatenate.73
  32.0 13.6 %gather_fusion = s32[2535]{0:T(1024)S(1)} fusion(s32[153664]{0:T(1024)S(1)} %reshape.586, s32[3072]{0:T(1024)S(1)} %pad_clamp_fusion.2), kind=kCustom, calls=%fused_computation | custom fusion | bytes 30420 | tf_op jit(solution)/shard_map/gather | solution.py:254
  45.8 12.3 %scatter_custom_fusion = s32[2535]{0:T(1024)S(1)} fusion(s32[2535]{0:T(1024)S(1)} %fusion.63, s32[2535]{0:T(1024)S(1)} %iota.255, s32[]{:T(128)} %constant.160.clone.1), kind=kCustom, calls=%fused_computation.211 | custom fusion | bytes 10144 | tf_op jit(solution)/shard_map/scatter | solution.py:612
  80.0 5.3 gather_fusion.1
  95.4 3.9 reshape.588
  102.6 6.0 reshape.589.cells_ref
  108.6 22.4 %bias_expand.1.bias_ref = f32[16,400,400]{2,1,0:T(8,128)} custom-call(bf16[16,56,1024]{2,1,0:T(8,128)(2,1)} %reshape.589.cells_ref, bf16[8,400,56]{2,1,0:T(8,128)(2,1)} %select_convert_fusion.rows_ref, bf16[512,400]{1,0:T(8,128)(2,1)} %select_convert_fusion.1.lanes_ref), custom_call_target="tpu_custom_call" | custom-call | tf_op jit(solution)/shard_map/bias_expand/pallas_call | solution.py:196
  168.6 4.5 multiply_convert_fusion
  174.7 34.9 %attention_forward.1 = (bf16[4,400,512]{2,1,0:T(8,128)(2,1)}, f32[4,400,512]{2,1,0:T(8,128)}, bf16[4,16,400,400]{3,2,1,0:T(8,128)(2,1)}) custom-call(bf16[4,400,1536]{2,1,0:T(8,128)(2,1)} %bitcast.215, bf16[4,400,1536]{2,1,0:T(8,128)(2,1)} %bitcast.216, bf16[4,400,1536]{2,1,0:T(8,128)(2,1)} %bitcast.217, bf16[4,400,128]{2,1,0:T(8,128)(2,1)} %bitcast.266, ...), custom_call_target="tpu_custom_call" | custom-call | tf_op jit(solution)/shard_map/attention_forward/pallas_call | solution.py:291
  211.4 4.8 fusion.78
  220.8 6.5 %reshape.599 = bf16[4,8,512,64]{3,2,1,0:T(8,128)(2,1)} reshape(bf16[4,8,256,128]{3,2,1,0:T(8,128)(2,1)} %get-tuple-element.138) | data formatting | bytes 4194304 | tf_op jit(solution)/shard_map/reshape | solution.py:502
  227.3 6.0 copy.317
  236.8 4.1 reshape.597
  246.5 34.0 %fusion.2 = (bf16[1600,2048]{1,0:T(8,128)(2,1)}, f32[1600,2048]{1,0:T(8,128)}) fusion(f32[2048]{0:T(1024)S(1)} %bitcast.277, bf16[512,2048]{1,0:T(8,128)(2,1)S(1)} %bitcast.261, f32[1600,512]{1,0:T(8,128)S(1)} %get-tuple-element.193, f32[512]{0:T(512)S(1)} %copy-done.68, f32[512]{0:T(512)S(1)} %copy-done.65, f32[1600]{0:T(1024)S(1)} %add_rsqrt_fusion, ...), kind=kOutput, calls=%fused_computation.8 | convolution fusion | flops 3575808000 | bytes 25059840 | tf_op jit(solution)/shard_map/dot_general | solution.py:531
  280.4 10.9 %fusion.89 = (f32[2048]{0:T(1024)S(1)}, bf16[1600,2048]{1,0:T(8,128)(2,1)S(1)}) fusion(f32[1600,2048]{1,0:T(8,128)} %get-tuple-element.195, f32[2048]{0:T(1024)S(1)} %bitcast.278, bf16[1600,512]{1,0:T(8,128)(2,1)S(1)} %bitcast.237, bf16[2048,512]{0,1:T(8,128)(2,1)S(1)} %bitcast.259), kind=kOutput, calls=%fused_computation.255 | convolution fusion | flops 3394762752 | bytes 23412736 | tf_op jit(solution)/shard_map/dot_general | solution.py:44
  291.4 4.8 multiply_reduce_fusion
  296.2 6.4 %fusion.20 = bf16[2048,512]{1,0:T(8,128)(2,1)} fusion(bf16[1600,2048]{1,0:T(8,128)(2,1)S(1)} %get-tuple-element.199, f32[1600,512]{1,0:T(8,128)S(1)} %get-tuple-element.193, f32[512]{0:T(512)S(1)} %copy-done.68, f32[512]{0:T(512)S(1)} %copy-done.65, f32[1600]{0:T(1024)S(1)} %add_rsqrt_fusion, f32[1600]{0:T(1024)S(1)} %broadcast_multiply_fusion.4), kind=kOutput, calls=%fused_computation.60 | convolution fusion | flops 3360587776 | bytes 11944448 | tf_op jit(solution)/shard_map/dot_general | solution.py:44
  308.3 57.5 %attention_backward.1 = (bf16[4,400,512]{2,1,0:T(8,128)(2,1)}, bf16[4,400,512]{2,1,0:T(8,128)(2,1)}, bf16[4,400,512]{2,1,0:T(8,128)(2,1)}, f32[16,400,400]{2,1,0:T(8,128)}) custom-call(bf16[4,400,1536]{2,1,0:T(8,128)(2,1)} %bitcast.218, bf16[4,400,1536]{2,1,0:T(8,128)(2,1)} %bitcast.219, bf16[4,400,1536]{2,1,0:T(8,128)(2,1)} %bitcast.220, ...), custom_call_target="tpu_custom_call" | custom-call | tf_op jit(solution)/shard_map/attention_backward/pallas_call | solution.py:366
  367.6 3.9 convolution_bitcast_fusion.2
  386.6 3.8 fusion.79
  394.3 7.1 %convolution_convert_fusion.2 = bf16[512,2048]{1,0:T(8,128)(2,1)S(1)} fusion(bf16[1600,512]{1,0:T(8,128)(2,1)S(1)} %bitcast.238, bf16[1600,2048]{1,0:T(8,128)(2,1)} %get-tuple-element.194), kind=kOutput, calls=%fused_computation.61 | convolution fusion | flops 3356491776 | bytes 10289152 | tf_op jit(solution)/shard_map/dot_general | solution.py:44
  406.8 3.9 copy.347
  412.5 5.9 pad_maximum_fusion
  418.5 32.2 %bias_collect.1 = f32[16,56,1024]{2,1,0:T(8,128)} custom-call(f32[16,400,400]{2,1,0:T(8,128)} %get-tuple-element.29.grad_ref, bf16[8,56,400]{2,1,0:T(8,128)(2,1)} %select_convert_fusion.2.rows_ref, bf16[400,512]{1,0:T(8,128)(2,1)} %select_convert_fusion.3.lanes_ref), custom_call_target="tpu_custom_call" | custom-call | tf_op jit(solution)/shard_map/bias_collect/pallas_call | solution.py:229
  450.6 4.0 copy.343
  463.6 9.1 %copy.344 = f32[16,15,49,64]{3,2,1,0:T(8,128)} copy(f32[16,15,49,64]{3,1,0,2:T(8,128)} %bitcast.223) | data formatting | bytes 6021120 | tf_op jit(solution)/shard_map/transpose | solution.py:576
  472.8 5.1 reshape.636
  488.7 7.2 %add_convert_fusion = bf16[1600,512]{1,0:T(8,128)(2,1)S(1)} fusion(f32[1600,512]{1,0:T(8,128)S(1)} %copy-done.6, bf16[1600,2048]{1,0:T(8,128)(2,1)} %get-tuple-element.194, bf16[2048,512]{0,1:T(8,128)(2,1)} %bitcast.258, f32[512]{0:T(512)S(1)} %copy-done.67), kind=kOutput, calls=%fused_computation.50 | convolution fusion | flops 3357900800 | bytes 13568000 | tf_op jit(solution)/shard_map/dot_general | solution.py:533
  539.2 7.5 %gather_fusion.2 = f32[2535,2]{1,0:T(8,128)} fusion(f32[2,2535]{0,1:T(8,128)} %copy.350, s32[3072]{0:T(1024)} %pad_clamp_fusion), kind=kCustom, calls=%fused_computation.2 | custom fusion | bytes 50700 | tf_op jit(solution)/shard_map/jit(_take)/gather | solution.py:613
  550.3 8.1 %collective-permute-done.21 = bf16[2,192,512]{2,1,0:T(8,128)(2,1)S(1)} collective-permute-done((bf16[2,192,512]{2,1,0:T(8,128)(2,1)S(1)}, bf16[2,192,512]{2,1,0:T(8,128)(2,1)S(1)}, u32[]{:S(2)}, u32[]{:S(2)}) %collective-permute-start.21) | collective-permute-done | bytes 393248 | tf_op jit(solution)/shard_map/ppermute | solution.py:49
  591.0 16.4 %collective-permute-done.24 = bf16[192,512]{1,0:T(8,128)(2,1)S(1)} collective-permute-done((bf16[192,512]{1,0:T(8,128)(2,1)S(1)}, bf16[192,512]{1,0:T(8,128)(2,1)S(1)}, u32[]{:S(2)}, u32[]{:S(2)}) %collective-permute-start.24) | collective-permute-done | bytes 196640 | tf_op jit(solution)/shard_map/ppermute | solution.py:49
  608.2 21.6 %all-reduce.7.cloned.1.call-done = bf16[576,512]{0,1:T(8,128)(2,1)} async-done(((bf16[576,512]{0,1:T(8,128)(2,1)}), bf16[576,512]{0,1:T(8,128)(2,1)}) %all-reduce.7.cloned.1.call-update) | async-done | bytes 589840 | tf_op jit(solution)/shard_map/psum | solution.py:560
  (454 shorter events, 245.8 us)
Async XLA Ops:
  7.2 202.4 %all-gather.3.cloned.1.call-start = ((), (), s32[]{:S(2)}) async-start(), calls=%async_computation.3 | async-start | bytes 4866048 | tf_op jit(solution)/shard_map/all_gather | solution.py:498
  14.1 52.6 %collective-permute-start.3 = (bf16[46,128]{1,0:T(8,128)(2,1)S(1)}, bf16[46,128]{1,0:T(8,128)(2,1)S(1)}, u32[]{:S(2)}, u32[]{:S(2)}) collective-permute-start(bf16[46,128]{1,0:T(8,128)(2,1)S(1)} %pad_bitcast_fusion), channel_id=1, source_target_pairs={{0,16},{8,24},{16,0},{24,8},{1,17},{9,25},{17,1},{25,9},{2,18},{10... | collective-permute-start | bytes 35336 | tf_op jit(solution)/shard_map/ppermute | solution.py:49
  17.1 58.0 %collective-permute-start.6 = (bf16[128,192]{0,1:T(8,128)(2,1)}, bf16[128,192]{0,1:T(8,128)(2,1)}, u32[]{:S(2)}, u32[]{:S(2)}) collective-permute-start(bf16[128,192]{0,1:T(8,128)(2,1)} %param.24), channel_id=1, source_target_pairs={{0,1},{1,0},{2,3},{3,2},{4,5},{5,4},{6,7},{7,6},{8,9},{9,8},{10,11... | collective-permute-start | bytes 147464 | tf_op jit(solution)/shard_map/ppermute | solution.py:49
  22.3 563.7 %reduce-scatter.2.cloned.1.call-start = ((), (), s32[]{:S(2)}) async-start(), calls=%async_computation.1 | async-start | bytes 5898240 | tf_op jit(solution)/shard_map/reduce_scatter | solution.py:560
  24.9 106.8 %collective-permute-start = (bf16[336,512]{1,0:T(8,128)(2,1)}, bf16[336,512]{1,0:T(8,128)(2,1)}, u32[]{:S(2)}, u32[]{:S(2)}) collective-permute-start(bf16[336,512]{1,0:T(8,128)(2,1)} %reshape.572), channel_id=1, source_target_pairs={{0,4},{4,0},{8,12},{12,8},{16,20},{20,16},{24,28},{28,24},{1,5},{5... | collective-permute-start | bytes 1032200 | tf_op jit(solution)/shard_map/ppermute | solution.py:114
  27.3 110.3 %collective-permute-start.2 = (bf16[336,512]{1,0:T(8,128)(2,1)}, bf16[336,512]{1,0:T(8,128)(2,1)}, u32[]{:S(2)}, u32[]{:S(2)}) collective-permute-start(bf16[336,512]{1,0:T(8,128)(2,1)} %reshape.576), channel_id=1, source_target_pairs={{0,28},{4,24},{8,4},{12,0},{16,12},{20,8},{24,20},{28,16},{1,29},{... | collective-permute-start | bytes 1032200 | tf_op jit(solution)/shard_map/ppermute | solution.py:114
  30.5 109.8 %collective-permute-start.14 = (bf16[336,512]{1,0:T(8,128)(2,1)}, bf16[336,512]{1,0:T(8,128)(2,1)}, u32[]{:S(2)}, u32[]{:S(2)}) collective-permute-start(bf16[336,512]{1,0:T(8,128)(2,1)} %reshape.609), channel_id=1, source_target_pairs={{0,4},{4,0},{8,12},{12,8},{16,20},{20,16},{24,28},{28,24},{1,5},{5... | collective-permute-start | bytes 1032200 | tf_op jit(solution)/shard_map/ppermute | solution.py:114
  66.8 7.9 %collective-permute-start.4 = (bf16[2,46,128]{2,1,0:T(8,128)(2,1)S(1)}, bf16[2,46,128]{2,1,0:T(8,128)(2,1)S(1)}, u32[]{:S(2)}, u32[]{:S(2)}) collective-permute-start(bf16[2,46,128]{2,1,0:T(8,128)(2,1)S(1)} %pad_maximum_fusion.25), channel_id=1, source_target_pairs={{0,4},{4,0},{1,5},{5,1},{2,6},{6,2},{3,7},{7,3},{8,12},{12,8},{9,1... | collective-permute-start | bytes 70664 | tf_op jit(solution)/shard_map/ppermute | solution.py:49
  74.7 68.0 %collective-permute-start.15 = (bf16[448,512]{1,0:T(8,128)(2,1)}, bf16[448,512]{1,0:T(8,128)(2,1)}, u32[]{:S(2)}, u32[]{:S(2)}) collective-permute-start(bf16[448,512]{1,0:T(8,128)(2,1)} %reshape.611), channel_id=1, source_target_pairs={{0,24},{4,28},{8,0},{12,4},{16,8},{20,12},{24,16},{28,20},{1,25},{... | collective-permute-start | bytes 1376264 | tf_op jit(solution)/shard_map/ppermute | solution.py:114
  76.8 12.5 %collective-permute-start.7 = (bf16[2,128,192]{1,2,0:T(8,128)(2,1)S(1)}, bf16[2,128,192]{1,2,0:T(8,128)(2,1)S(1)}, u32[]{:S(2)}, u32[]{:S(2)}) collective-permute-start(bf16[2,128,192]{1,2,0:T(8,128)(2,1)S(1)} %pad_maximum_fusion.23), channel_id=1, source_target_pairs={{0,2},{1,3},{2,0},{3,1},{4,6},{5,7},{6,4},{7,5},{8,10},{9,11},{10,... | collective-permute-start | bytes 294920 | tf_op jit(solution)/shard_map/ppermute | solution.py:49
  90.6 43.6 %collective-permute-start.8 = (bf16[2,2,128,192]{2,3,1,0:T(8,128)(2,1)}, bf16[2,2,128,192]{2,3,1,0:T(8,128)(2,1)}, u32[]{:S(2)}, u32[]{:S(2)}) collective-permute-start(bf16[2,2,128,192]{2,3,1,0:T(8,128)(2,1)} %pad_maximum_fusion.21), channel_id=1, source_target_pairs={{0,16},{8,24},{16,0},{24,8},{1,17},{9,25},{17,1},{25,9},{2,18},{10... | collective-permute-start | bytes 589832 | tf_op jit(solution)/shard_map/ppermute | solution.py:49
  131.6 11.0 %collective-permute-start.16 = (bf16[336,512]{1,0:T(8,128)(2,1)S(1)}, bf16[336,512]{1,0:T(8,128)(2,1)S(1)}, u32[]{:S(2)}, u32[]{:S(2)}) collective-permute-start(bf16[336,512]{1,0:T(8,128)(2,1)S(1)} %copy-done.45), channel_id=1, source_target_pairs={{0,28},{4,24},{8,4},{12,0},{16,12},{20,8},{24,20},{28,16},{1,29},{... | collective-permute-start | bytes 1032200 | tf_op jit(solution)/shard_map/ppermute | solution.py:114
  134.3 17.0 %collective-permute-start.1 = (bf16[448,512]{1,0:T(8,128)(2,1)}, bf16[448,512]{1,0:T(8,128)(2,1)}, u32[]{:S(2)}, u32[]{:S(2)}) collective-permute-start(bf16[448,512]{1,0:T(8,128)(2,1)} %reshape.574), channel_id=1, source_target_pairs={{0,24},{4,28},{8,0},{12,4},{16,8},{20,12},{24,16},{28,20},{1,25},{... | collective-permute-start | bytes 1376264 | tf_op jit(solution)/shard_map/ppermute | solution.py:114
  137.6 19.4 %collective-permute-start.9 = (bf16[2,2,2,128,192]{3,4,0,2,1:T(8,128)(2,1)}, bf16[2,2,2,128,192]{3,4,0,2,1:T(8,128)(2,1)}, u32[]{:S(2)}, u32[]{:S(2)}) collective-permute-start(bf16[2,2,2,128,192]{3,4,0,2,1:T(8,128)(2,1)} %pad_maximum_fusion.18), channel_id=1, source_target_pairs={{0,4},{4,0},{1,5},{5,1},{2,6},{6,2},{3,7},{7,3},{8,12},{12,8},{9,1... | collective-permute-start | bytes 1179656 | tf_op jit(solution)/shard_map/ppermute | solution.py:49
  159.8 4.3 collective-permute-start.10
  418.4 211.4 %all-reduce.7.cloned.1.call-start = ((), (), s32[]{:S(2)}) async-start(), calls=%async_computation.2 | async-start | bytes 1310720 | tf_op jit(solution)/shard_map/psum | solution.py:560
  459.5 87.2 %collective-permute-start.20 = (bf16[2,2,192,512]{3,2,0,1:T(8,128)(2,1)}, bf16[2,2,192,512]{3,2,0,1:T(8,128)(2,1)}, u32[]{:S(2)}, u32[]{:S(2)}) collective-permute-start(bf16[2,2,192,512]{3,2,0,1:T(8,128)(2,1)} %fusion.42), channel_id=1, source_target_pairs={{0,8},{8,0},{16,24},{24,16},{1,9},{9,1},{17,25},{25,17},{2,10},{10... | collective-permute-start | bytes 2359304 | tf_op jit(solution)/shard_map/ppermute | solution.py:49
  485.7 14.5 %collective-permute-start.25 = (f32[2,2,46,128]{3,2,1,0:T(8,128)}, f32[2,2,46,128]{3,2,1,0:T(8,128)}, u32[]{:S(2)}, u32[]{:S(2)}) collective-permute-start(f32[2,2,46,128]{3,2,1,0:T(8,128)} %dynamic-slice_bitcast_fusion), channel_id=1, source_target_pairs={{0,8},{8,0},{16,24},{24,16},{1,9},{9,1},{17,25},{25,17},{2,10},{10... | collective-permute-start | bytes 282632 | tf_op jit(solution)/shard_map/ppermute | solution.py:49
  501.3 4.2 collective-permute-start.26
  505.5 3.9 collective-permute-start.27
  509.4 3.8 collective-permute-start.28
  513.2 21.6 %collective-permute-start.29 = (f32[46,128]{1,0:T(8,128)S(1)}, f32[46,128]{1,0:T(8,128)S(1)}, u32[]{:S(2)}, u32[]{:S(2)}) collective-permute-start(f32[46,128]{1,0:T(8,128)S(1)} %add.365), channel_id=1, source_target_pairs={{0,2},{1,3},{2,0},{3,1},{4,6},{5,7},{6,4},{7,5},{8,10},{9,11},{10,... | collective-permute-start | bytes 70664 | tf_op jit(solution)/shard_map/ppermute | solution.py:49
  517.6 41.6 %collective-permute-start.11 = (bf16[336,512]{1,0:T(8,128)(2,1)}, bf16[336,512]{1,0:T(8,128)(2,1)}, u32[]{:S(2)}, u32[]{:S(2)}) collective-permute-start(bf16[336,512]{1,0:T(8,128)(2,1)} %reshape.603), channel_id=1, source_target_pairs={{0,12},{4,8},{8,20},{12,16},{16,28},{20,24},{24,4},{28,0},{1,13},{... | collective-permute-start | bytes 1032200 | tf_op jit(solution)/shard_map/ppermute | solution.py:114
  518.8 46.0 %collective-permute-start.13 = (bf16[336,512]{1,0:T(8,128)(2,1)}, bf16[336,512]{1,0:T(8,128)(2,1)}, u32[]{:S(2)}, u32[]{:S(2)}) collective-permute-start(bf16[336,512]{1,0:T(8,128)(2,1)} %reshape.607), channel_id=1, source_target_pairs={{0,4},{4,0},{8,12},{12,8},{16,20},{20,16},{24,28},{28,24},{1,5},{5... | collective-permute-start | bytes 1032200 | tf_op jit(solution)/shard_map/ppermute | solution.py:114
  529.5 38.0 %collective-permute-start.17 = (bf16[336,512]{1,0:T(8,128)(2,1)}, bf16[336,512]{1,0:T(8,128)(2,1)}, u32[]{:S(2)}, u32[]{:S(2)}) collective-permute-start(bf16[336,512]{1,0:T(8,128)(2,1)} %reshape.623), channel_id=1, source_target_pairs={{0,12},{4,8},{8,20},{12,16},{16,28},{20,24},{24,4},{28,0},{1,13},{... | collective-permute-start | bytes 1032200 | tf_op jit(solution)/shard_map/ppermute | solution.py:114
  535.5 33.4 %collective-permute-start.19 = (bf16[336,512]{1,0:T(8,128)(2,1)}, bf16[336,512]{1,0:T(8,128)(2,1)}, u32[]{:S(2)}, u32[]{:S(2)}) collective-permute-start(bf16[336,512]{1,0:T(8,128)(2,1)} %reshape.625), channel_id=1, source_target_pairs={{0,4},{4,0},{8,12},{12,8},{16,20},{20,16},{24,28},{28,24},{1,5},{5... | collective-permute-start | bytes 1032200 | tf_op jit(solution)/shard_map/ppermute | solution.py:114
  548.3 10.1 %collective-permute-start.21 = (bf16[2,192,512]{2,1,0:T(8,128)(2,1)S(1)}, bf16[2,192,512]{2,1,0:T(8,128)(2,1)S(1)}, u32[]{:S(2)}, u32[]{:S(2)}) collective-permute-start(bf16[2,192,512]{2,1,0:T(8,128)(2,1)S(1)} %fusion.59), channel_id=1, source_target_pairs={{0,4},{4,0},{1,5},{5,1},{2,6},{6,2},{3,7},{7,3},{8,12},{12,8},{9,1... | collective-permute-start | bytes 1179656 | tf_op jit(solution)/shard_map/ppermute | solution.py:49
  558.4 13.0 %collective-permute-start.18 = (bf16[448,512]{1,0:T(8,128)(2,1)}, bf16[448,512]{1,0:T(8,128)(2,1)S(1)}, u32[]{:S(2)}, u32[]{:S(2)}) collective-permute-start(bf16[448,512]{1,0:T(8,128)(2,1)} %reshape.624), channel_id=1, source_target_pairs={{0,8},{4,12},{8,16},{12,20},{16,24},{20,28},{24,0},{28,4},{1,9},{5... | collective-permute-start | bytes 1376264 | tf_op jit(solution)/shard_map/ppermute | solution.py:114
  559.2 13.7 %collective-permute-start.22 = (bf16[192,512]{1,0:T(8,128)(2,1)}, bf16[192,512]{1,0:T(8,128)(2,1)}, u32[]{:S(2)}, u32[]{:S(2)}) collective-permute-start(bf16[192,512]{1,0:T(8,128)(2,1)} %fusion.61), channel_id=1, source_target_pairs={{0,16},{8,24},{16,0},{24,8},{1,17},{9,25},{17,1},{25,9},{2,18},{10... | collective-permute-start | bytes 589832 | tf_op jit(solution)/shard_map/ppermute | solution.py:49
  564.7 14.4 %collective-permute-start.12 = (bf16[448,512]{1,0:T(8,128)(2,1)}, bf16[448,512]{1,0:T(8,128)(2,1)}, u32[]{:S(2)}, u32[]{:S(2)}) collective-permute-start(bf16[448,512]{1,0:T(8,128)(2,1)} %reshape.605), channel_id=1, source_target_pairs={{0,8},{4,12},{8,16},{12,20},{16,24},{20,28},{24,0},{28,4},{1,9},{5... | collective-permute-start | bytes 1376264 | tf_op jit(solution)/shard_map/ppermute | solution.py:114
  574.6 11.4 %collective-permute-start.23 = (bf16[192,512]{1,0:T(8,128)(2,1)}, bf16[192,512]{1,0:T(8,128)(2,1)}, u32[]{:S(2)}, u32[]{:S(2)}) collective-permute-start(bf16[192,512]{1,0:T(8,128)(2,1)} %fusion.60), channel_id=1, source_target_pairs={{0,1},{1,0},{2,3},{3,2},{4,5},{5,4},{6,7},{7,6},{8,9},{9,8},{10,11... | collective-permute-start | bytes 589832 | tf_op jit(solution)/shard_map/ppermute | solution.py:49
  587.1 20.3 %collective-permute-start.24 = (bf16[192,512]{1,0:T(8,128)(2,1)S(1)}, bf16[192,512]{1,0:T(8,128)(2,1)S(1)}, u32[]{:S(2)}, u32[]{:S(2)}) collective-permute-start(bf16[192,512]{1,0:T(8,128)(2,1)S(1)} %add_convert_fusion.3), channel_id=1, source_target_pairs={{0,2},{1,3},{2,0},{3,1},{4,6},{5,7},{6,4},{7,5},{8,10},{9,11},{10,... | collective-permute-start | bytes 589832 | tf_op jit(solution)/shard_map/ppermute | solution.py:49
  (74 other events, 1052.1 us)
Sparse Core Ops, SparseCore 0:
  22.4 69.0 all-gather.2
  418.5 55.1 reduce-scatter.1
  586.1 43.6 all-reduce.6
